TPU v7x, 32 devices: a whole 2x2x4 slice. The times are simulated.
32 devices in a mesh: px: 4 (over z), py: 8 (over y, x, core).
Axes of the slice: x: 2, y: 2, z: 4, core: 2. Of those that a mesh axis runs over, the one named last changes fastest.
Arguments:
- current_state: float32 [5, 125, 32768], P(None, None, ('px', 'py')), may hold values from -6 to 6
- state_old: float32 [5, 125, 32768], P(None, None, ('px', 'py')), may hold values from -6 to 6
- jacobian: float32 [32768], P(('px', 'py')), may hold values from 0.5 to 2
- volume_operator_list: float32 [3, 125, 125], replicated, may hold values from -0.3125 to 0.3125
- flux_jacobian_list: float32 [3, 5, 5], replicated, may hold values from -2.5 to 2.5
- penalty: float32 [5], replicated, may hold values from 0.5 to 2
- cut_owner: int32 [1280, 1], P(('px', 'py')), may hold values from 0 to 7; in each aligned block of 40 rows (0 to 39, 40 to 79, ...) at most 8 rows name the same one
- cut_element: int32 [1280], P(('px', 'py')), may hold values from 0 to 1023
- cut_mass: float32 [1280, 125, 125], P(('px', 'py')), may hold values from -0.5 to 0.5
- cut_operator: float32 [1280, 125, 125], P(('px', 'py')), may hold values from -0.5 to 0.5
- body_holder_index: int32 [24], P('px'), may hold values from 0 to 7
- body_points: float32 [192, 3, 128], P(('px', 'py')), may hold values from -1 to 1
- body_normals: float32 [192, 3, 128], P(('px', 'py')), may hold values from -6 to 6
- body_weights: float32 [192, 128], P(('px', 'py')), may hold values from 0.01 to 0.1
- covered: int32 [192, 16], P(('px', 'py')), may hold values from 0 to 1023
Outputs:
- residual: float32 [5, 125, 32768], P(None, None, ('px', 'py'))
Inputs may be any that keep to these rules, and one draw needn't show every extreme that they name: `cut_owner`: among the 40 rows of one device no owner is named by more than 8 rows, a bound that some block reaches. Owners are py indices within the same slab. `cut_element`: several cut blocks may belong to one element; their terms add. `body_holder_index`: only the slot of the owning device is read for each body. `covered`: an element may be listed more than once; its terms add.
All inputs are finite; a program needn't handle non-finite values.
Results may differ from a plain program's by a relative error of at most 0.0001.
Values sent between devices are 32-bit elements; how exact they have to be, the bound alone decides.
No kernel may reach another device: no remote copies, remote signals or barrier semaphores. Data moves between devices by JAX's collectives and lax.ppermute only.
A program may use at most 128 MiB of HBM per device.

v0:
```python
import functools

import jax
import jax.numpy as jnp
from jax import lax
from jax.experimental import pallas as pl
from jax.experimental.pallas import tpu as pltpu
from jax.sharding import PartitionSpec as P

DEGREE = 4
LAYERS = 8
LANES = 128
SUBS = 8
MIB = 1 << 20

F32 = jnp.float32
BF16 = jnp.bfloat16
NN = (((1,), (0,)), ((), ()))
NT = (((1,), (1,)), ((), ()))


def pad8(count):
    return -(-count // SUBS) * SUBS


def iota(shape, dim):
    return lax.broadcasted_iota(jnp.int32, shape, dim)


def halves(value):
    high = value.astype(BF16)
    return high, (value - high.astype(F32)).astype(BF16)


def mxu(left, right, dims=NN):
    return lax.dot_general(left, right, dims, preferred_element_type=F32)


def product(left, right, dims=NN):
    left_high, left_low = left
    right_high, right_low = right
    return mxu(left_high, right_high, dims) + (
        mxu(left_low, right_high, dims) + mxu(left_high, right_low, dims)
    )


def exact_dot(left, right):
    return lax.dot_general(
        left, right, NN, precision=lax.Precision.HIGHEST, preferred_element_type=F32
    )


def pick_lanes(values, lanes):
    return jnp.take_along_axis(values, jnp.broadcast_to(lanes, values.shape), axis=1)


def params(limit):
    return pltpu.CompilerParams(vmem_limit_bytes=limit * MIB)


def whole(array):
    return pl.BlockSpec(array.shape, lambda *_: (0,) * array.ndim)


def smem():
    return pl.BlockSpec(memory_space=pltpu.SMEM)


def ids_kernel(cap, share, hold_ref, owner_ref, elem_ref, points_ref, normals_ref, weights_ref, out_ref, rows_ref):
    peers = out_ref.shape[0]
    bodies = points_ref.shape[0]
    cuts = owner_ref.shape[0]
    me = lax.axis_index("py")
    owner = owner_ref[...]
    named = (owner == iota((cuts, LANES), 1)).astype(F32)
    earlier = (iota((cuts, cuts), 1) < iota((cuts, cuts), 0)).astype(F32)
    place = jnp.sum(mxu(earlier, named) * named, axis=1, keepdims=True).astype(jnp.int32)
    placing = (owner * cap + place == iota((cuts, LANES), 1)).astype(F32)
    ids = exact_dot(elem_ref[...].astype(F32) + 1.0, placing) - 1.0
    rows_ref[...] = jnp.zeros_like(rows_ref)
    for body in range(bodies):
        mine = hold_ref[body] == me
        rows_ref[body * 7 : body * 7 + 3] = jnp.where(mine, points_ref[body], 0.0)
        rows_ref[body * 7 + 3 : body * 7 + 6] = jnp.where(mine, normals_ref[body], 0.0)
        rows_ref[body * 7 + 6 : body * 7 + 7] = jnp.where(mine, weights_ref[body : body + 1], 0.0)
    for peer in range(peers):
        out_ref[peer] = jnp.zeros((SUBS, LANES), F32)
        out_ref[peer, 0:1] = ids
        out_ref[peer, 1 : 1 + share] = rows_ref[peer * share : (peer + 1) * share]


def rim_kernel(state_ref, covered_ref, low_ref, up_ref, rows_ref, column_ref, lane_ref, acc_ref):
    step = pl.program_id(0)
    nvar, modes, _ = state_ref.shape
    face = modes // (DEGREE + 1)
    bodies, count = covered_ref.shape

    @pl.when(step == 0)
    def _():
        spread = (iota((count, LANES), 1) % count == iota((count, LANES), 0)).astype(F32)
        tiled = exact_dot(covered_ref[...].astype(F32), spread)
        kept = jnp.where(iota((bodies, LANES), 1) // count == iota((bodies, LANES), 0), tiled + 1.0, 0.0)
        row = jnp.sum(kept, axis=0, keepdims=True) - 1.0
        spot = jnp.broadcast_to(row, (LANES, LANES))
        column_ref[...] = spot.T.astype(jnp.int32)
        lane_ref[...] = row.astype(jnp.int32)
        acc_ref[...] = jnp.zeros_like(acc_ref)

    def sums(var):
        part = [state_ref[var, i * face : (i + 1) * face, :] for i in range(DEGREE + 1)]
        return (part[0] + part[2]) + part[4], part[1] + part[3]

    @pl.when(step == 0)
    def _():
        for var in range(nvar):
            even, odd = sums(var)
            low_ref[var] = jnp.zeros(low_ref.shape[1:], F32)
            low_ref[var, :face] = even - odd

    @pl.when(step == pl.num_programs(0) - 1)
    def _():
        for var in range(nvar):
            even, odd = sums(var)
            up_ref[var] = jnp.zeros(up_ref.shape[1:], F32)
            up_ref[var, :face] = even + odd

    spots = lane_ref[...]
    here = spots // LANES == step
    for var in range(nvar):
        found = pick_lanes(state_ref[var], spots % LANES)
        acc_ref[var, :modes] = jnp.where(here, found, acc_ref[var, :modes])

    @pl.when(step == pl.num_programs(0) - 1)
    def _():
        for var in range(nvar):
            rows_ref[var] = acc_ref[var].T


def pick_kernel(cap, share, got_ref, state_ref, old_ref, out_ref, column_ref, lane_ref, acc_ref):
    step = pl.program_id(0)
    nvar, modes, _ = state_ref.shape
    peers = got_ref.shape[0]
    half = LANES // 2
    lane = iota((1, LANES), 1)

    @pl.when(step == 0)
    def _():
        me = lax.axis_index("py")
        row = jnp.zeros((1, LANES), F32) - 1.0
        for peer in range(peers):
            moved = pltpu.roll(got_ref[peer, 0:1], ((peer - me) * cap + LANES) % LANES, 1)
            row = jnp.where(lane // cap == peer, moved, row)
        row = jnp.where(lane < half, row, pltpu.roll(row, half, 1))
        column_ref[...] = jnp.broadcast_to(row, (LANES, LANES)).T.astype(jnp.int32)
        lane_ref[...] = row.astype(jnp.int32)
        acc_ref[...] = jnp.zeros_like(acc_ref)
        data = got_ref[0]
        for peer in range(1, peers):
            data = data + got_ref[peer]
        for peer in range(peers):
            out_ref[peer, 2 * nvar, :, :] = data

    spots = lane_ref[...]
    here = (spots + LANES) // LANES == step + 1
    for var in range(nvar):
        found = jnp.where(
            lane < half,
            pick_lanes(state_ref[var], spots & (LANES - 1)),
            pick_lanes(old_ref[var], spots & (LANES - 1)),
        )
        acc_ref[var, :modes] = jnp.where(here, found, acc_ref[var, :modes])

    @pl.when(step == pl.num_programs(0) - 1)
    def _():
        for var in range(nvar):
            rows = acc_ref[var].T
            for peer in range(peers):
                for kind in range(2):
                    first = kind * half + peer * cap
                    if cap < SUBS:
                        out_ref[peer, kind * nvar + var] = jnp.zeros((SUBS, LANES), F32)
                    out_ref[peer, kind * nvar + var, :cap] = rows[first : first + cap]


def main_kernel(
    flux_ref, penalty_ref, state_ref, under_ref, over_ref, old_ref, jac_ref, below_ref, above_ref, operator_ref,
    out_ref, matrix_ref, right_ref, face_ref,
):
    step = pl.program_id(0)
    steps = pl.num_programs(0)
    nvar, modes, width = state_ref.shape
    degree_one = DEGREE + 1
    face = modes // degree_one
    size = nvar * LANES

    @pl.when(step == 0)
    def _():
        matrix_ref[...] = jnp.zeros_like(matrix_ref)
        right_ref[...] = jnp.zeros_like(right_ref)
        face_ref[...] = jnp.zeros_like(face_ref)
        row, col = iota((modes, modes), 0), iota((modes, modes), 1)
        paired = (row % face == col % face) & ((row // face + col // face) % 2 == 0)
        own_face = jnp.where(paired, 2.0, 0.0).astype(F32)
        for var in range(nvar):
            for other in range(nvar):
                block = -(flux_ref[0, var, other] * operator_ref[0])
                for direction in range(1, 3):
                    block = block - flux_ref[direction, var, other] * operator_ref[direction]
                if var == other:
                    block = block + penalty_ref[var] * own_face
                high, low = halves(block)
                rows = slice(var * LANES, var * LANES + modes)
                for place, part in ((0, high), (size, high), (2 * size, low)):
                    matrix_ref[rows, place + other * LANES : place + other * LANES + modes] = part

    for var in range(nvar):
        high, low = halves(state_ref[var])
        rows = slice(var * LANES, var * LANES + modes)
        for place, part in ((0, high), (size, low), (2 * size, high)):
            right_ref[place + var * LANES : place + var * LANES + modes] = part

    product_now = mxu(matrix_ref[...], right_ref[...])
    mode = iota((modes, width), 0)
    weight = 8.0 / (
        (2.0 * (mode // (degree_one * degree_one)).astype(F32) + 1.0)
        * (2.0 * (mode // degree_one % degree_one).astype(F32) + 1.0)
        * (2.0 * (mode % degree_one).astype(F32) + 1.0)
    )
    scale = weight * jac_ref[...]

    def sums(ref, var):
        part = [ref[var, i * face : (i + 1) * face, :] for i in range(degree_one)]
        return (part[0] + part[2]) + part[4], part[1] + part[3]

    for var in range(nvar):
        even, odd = sums(state_ref, var)
        upper, lower = even + odd, even - odd
        even, odd = sums(over_ref, var)
        above = jnp.where(step == steps - 1, above_ref[var, :face], even - odd)
        even, odd = sums(under_ref, var)
        below = jnp.where(step == 0, below_ref[var, :face], even + odd)
        above = jnp.concatenate([lower[:, LANES:], above], axis=1)
        below = jnp.concatenate([below, upper[:, : width - LANES]], axis=1)
        plus = penalty_ref[var] * (above + below)
        minus = penalty_ref[var] * (above - below)
        for i in range(degree_one):
            face_ref[i * face : (i + 1) * face] = minus if i % 2 else plus
        change = state_ref[var] - old_ref[var]
        out_ref[var] = (
            product_now[var * LANES : var * LANES + modes] + scale * change
        ) - face_ref[:modes]


def cut_kernel(owner_ref, got_ref, mass_ref, operator_ref, out_ref, seen_ref, columns_ref):
    step = pl.program_id(0)
    block, modes, _ = mass_ref.shape
    peers, nvar = out_ref.shape[0], out_ref.shape[1]

    @pl.when(step == 0)
    def _():
        out_ref[...] = jnp.zeros_like(out_ref)
        for peer in range(peers):
            seen_ref[peer] = 0

    lane = iota((modes, LANES), 1)
    columns = jnp.zeros((modes, LANES), F32)
    spots = []
    for index in range(block):
        owner = owner_ref[step * block + index]
        place = seen_ref[owner]
        seen_ref[owner] = place + 1
        spots.append((owner, place))
        for var in range(nvar):
            state = got_ref[owner, var, pl.ds(place, 1), :]
            change = state - got_ref[owner, nvar + var, pl.ds(place, 1), :]
            term = mass_ref[index] * change[:, :modes] - operator_ref[index] * state[:, :modes]
            total = jnp.sum(term, axis=1, keepdims=True)
            columns = jnp.where(lane == index * nvar + var, total, columns)
    columns_ref[...] = jnp.zeros_like(columns_ref)
    columns_ref[:modes] = columns
    rows = columns_ref[...].T
    for index, (owner, place) in enumerate(spots):
        for var in range(nvar):
            first = index * nvar + var
            out_ref[owner, var, pl.ds(place, 1), :] = rows[first : first + 1]


def body_kernel(bodies, count, share, got_ref, rows_ref, column_ref, base_ref, out_ref, data_ref, lift_ref, left_ref):
    step = pl.program_id(0)
    peers = got_ref.shape[0]
    nvar, modes, width = out_ref.shape
    degree_one = DEGREE + 1

    @pl.when(step == 0)
    def _():
        for peer in range(peers):
            data_ref[peer * share : (peer + 1) * share] = got_ref[peer, 0, 1 : 1 + share]
        lift_ref[...] = jnp.zeros_like(lift_ref)
        mode, degree = iota((LANES, SUBS), 0), iota((LANES, SUBS), 1)
        real = mode < modes
        spreads = []
        for digit in (mode // (degree_one * degree_one), mode // degree_one % degree_one, mode % degree_one):
            chosen = (real & (digit == degree)).astype(BF16)
            spreads.append(jnp.concatenate([chosen, chosen, chosen], axis=1))
        ones = jnp.ones((1, LANES), F32)
        none = jnp.zeros((SUBS - degree_one, LANES), F32)
        for body in range(bodies):
            basis = None
            for axis in range(3):
                coords = data_ref[body * 7 + axis : body * 7 + axis + 1]
                table = [ones, coords]
                for n in range(1, DEGREE):
                    table.append(((2.0 * n + 1.0) * coords * table[n] - n * table[n - 1]) / (n + 1.0))
                stacked = jnp.concatenate(table + [none], axis=0)
                high = stacked.astype(BF16)
                rest = stacked - high.astype(F32)
                middle, low = halves(rest)
                factor = mxu(spreads[axis], jnp.concatenate([high, middle, low], axis=0))
                basis = factor if basis is None else basis * factor
            basis = halves(basis)
            rows = jnp.concatenate(
                [rows_ref[var, body * count : (body + 1) * count] for var in range(nvar)], axis=0
            )
            trace = product(halves(rows), basis)
            trace = [trace[var * count : (var + 1) * count] for var in range(nvar)]
            normal = [data_ref[body * 7 + 3 + axis : body * 7 + 4 + axis] for axis in range(3)]
            weights = data_ref[body * 7 + 6 : body * 7 + 7]
            speed = normal[0] * trace[1] + normal[1] * trace[2] + normal[2] * trace[3]
            flux = [speed + 0.5 * trace[0]] + [normal[axis] * trace[4] for axis in range(3)] + [1.4 * speed]
            weighted = jnp.concatenate([part * weights for part in flux], axis=0)
            lifted = product(halves(weighted), basis, NT)
            for var in range(nvar):
                lift_ref[var, body * count : (body + 1) * count] = lifted[var * count : (var + 1) * count]
        for var in range(nvar):
            high, low = halves(lift_ref[var].T)
            left_ref[var * LANES : (var + 1) * LANES, :LANES] = high
            left_ref[var * LANES : (var + 1) * LANES, LANES:] = low

    spots = jnp.concatenate([column_ref[...]] * (width // LANES), axis=1)
    chosen = (spots == iota((LANES, width), 1) + step * width).astype(BF16)
    added = mxu(left_ref[...], jnp.concatenate([chosen, chosen], axis=0))
    for var in range(nvar):
        out_ref[var] = base_ref[var] - added[var * LANES : var * LANES + modes]


def last_kernel(cap, got_ref, column_ref, base_ref, out_ref, slots_ref, left_ref):
    step = pl.program_id(0)
    peers = got_ref.shape[0]
    nvar, modes, width = out_ref.shape
    half = LANES // 2

    @pl.when(step == 0)
    def _():
        slots_ref[...] = jnp.zeros_like(slots_ref)
        for var in range(nvar):
            for peer in range(peers):
                slots_ref[peer * cap : (peer + 1) * cap] = got_ref[peer, var, :cap]
            high, low = halves(slots_ref[...].T)
            left_ref[var * LANES : (var + 1) * LANES, :half] = high[:, :half]
            left_ref[var * LANES : (var + 1) * LANES, half:] = low[:, :half]

    spots = jnp.concatenate([column_ref[...]] * (width // LANES), axis=1)
    chosen = (spots == iota((LANES, width), 1) + step * width).astype(BF16)
    added = mxu(left_ref[...], chosen)
    for var in range(nvar):
        out_ref[var] = base_ref[var] + added[var * LANES : var * LANES + modes]


def shift(value, axis, step):
    count = lax.axis_size(axis)
    pairs = [(source, source + step) for source in range(count) if 0 <= source + step < count]
    return lax.ppermute(value, axis, pairs)


def exchange(value):
    return lax.all_to_all(value, "py", split_axis=0, concat_axis=0, tiled=True)


def local(
    current_state, state_old, jacobian, volume_operator_list, flux_jacobian_list, penalty, cut_owner, cut_element,
    cut_mass, cut_operator, body_holder_index, body_points, body_normals, body_weights, covered,
):
    nvar, modes, elems = current_state.shape
    columns = elems // LAYERS
    face = modes // (DEGREE + 1)
    peers = lax.axis_size("py")
    cuts = cut_owner.shape[0]
    bodies, count = covered.shape
    cap = max(2, cuts * 3 // (2 * peers) + 1)
    share = -(-bodies * 7 // peers)
    half = LANES // 2
    assert columns == LANES and peers * cap <= half and bodies * count <= LANES
    assert cap <= SUBS and 1 + share <= SUBS and modes <= LANES
    shaped = jax.ShapeDtypeStruct
    wide = 2 * LANES
    steps = elems // wide
    layer = pl.BlockSpec((nvar, modes, LANES), lambda step: (0, 0, step))
    chunk = pl.BlockSpec((nvar, modes, wide), lambda step: (0, 0, step))

    asked = pl.pallas_call(
        functools.partial(ids_kernel, cap, share),
        out_shape=shaped((peers, SUBS, LANES), F32),
        in_specs=[smem()] + [pl.BlockSpec(memory_space=pltpu.VMEM)] * 5,
        out_specs=pl.BlockSpec(memory_space=pltpu.VMEM),
        scratch_shapes=[pltpu.VMEM((pad8(peers * share), LANES), F32)],
        compiler_params=params(8),
        name="ids",
    )(body_holder_index, cut_owner, cut_element.reshape(1, cuts), body_points, body_normals, body_weights)
    requests = exchange(asked)

    face_rows = shaped((nvar, pad8(face), LANES), F32)
    square = shaped((LANES, LANES), jnp.int32)
    stack = shaped((nvar, LANES, LANES), F32)
    lower, upper, covered_rows, covered_column = pl.pallas_call(
        rim_kernel,
        grid=(LAYERS,),
        out_shape=(face_rows, face_rows, stack, square),
        in_specs=[layer, whole(covered)],
        out_specs=(whole(face_rows), whole(face_rows), whole(stack), whole(square)),
        scratch_shapes=[pltpu.VMEM((1, LANES), jnp.int32), pltpu.VMEM(stack.shape, F32)],
        compiler_params=params(8),
        name="rim",
    )(current_state, covered)
    above_rim = shift(lower, "px", -1)
    below_rim = shift(upper, "px", 1)

    reply = shaped((peers, 2 * nvar + 1, SUBS, LANES), F32)
    states_out, slot_column = pl.pallas_call(
        functools.partial(pick_kernel, cap, share),
        grid=(LAYERS,),
        out_shape=(reply, square),
        in_specs=[whole(requests), layer, layer],
        out_specs=(whole(reply), whole(square)),
        scratch_shapes=[pltpu.VMEM((1, LANES), jnp.int32), pltpu.VMEM(stack.shape, F32)],
        compiler_params=params(8),
        name="pick",
    )(requests, current_state, state_old)
    replies = exchange(states_out)

    out = shaped(current_state.shape, F32)
    size = nvar * LANES
    residual = pl.pallas_call(
        main_kernel,
        grid=(steps,),
        out_shape=out,
        in_specs=[
            smem(),
            smem(),
            chunk,
            pl.BlockSpec((nvar, modes, LANES), lambda step: (0, 0, jnp.maximum(2 * step - 1, 0))),
            pl.BlockSpec((nvar, modes, LANES), lambda step: (0, 0, jnp.minimum(2 * step + 2, LAYERS - 1))),
            chunk,
            pl.BlockSpec((1, wide), lambda step: (0, step)),
            whole(below_rim),
            whole(above_rim),
            whole(volume_operator_list),
        ],
        out_specs=chunk,
        scratch_shapes=[
            pltpu.VMEM((size, 3 * size), BF16),
            pltpu.VMEM((3 * size, wide), BF16),
            pltpu.VMEM((LANES, wide), F32),
        ],
        compiler_params=params(24),
        cost_estimate=pl.CostEstimate(
            flops=6 * size * size * elems, transcendentals=0, bytes_accessed=4 * 4 * nvar * modes * elems
        ),
        name="main",
    )(
        flux_jacobian_list, penalty, current_state, current_state, current_state, state_old,
        jacobian.reshape(1, elems), below_rim, above_rim, volume_operator_list,
    )

    group = next(size for size in (8, 10, 5, 4, 2, 1) if cuts % size == 0)
    terms = shaped((peers, nvar, SUBS, LANES), F32)
    blocks = pl.BlockSpec((group, modes, modes), lambda step: (step, 0, 0))
    results_out = pl.pallas_call(
        cut_kernel,
        grid=(cuts // group,),
        out_shape=terms,
        in_specs=[smem(), whole(replies), blocks, blocks],
        out_specs=whole(terms),
        scratch_shapes=[pltpu.SMEM((peers,), jnp.int32), pltpu.VMEM((LANES, LANES), F32)],
        compiler_params=params(12),
        name="cut",
    )(cut_owner.reshape(cuts), replies, cut_mass, cut_operator)
    results = exchange(results_out)

    residual = pl.pallas_call(
        functools.partial(body_kernel, bodies, count, share),
        grid=(steps,),
        out_shape=out,
        in_specs=[
            pl.BlockSpec((peers, 1, SUBS, LANES), lambda step: (0, 2 * nvar, 0, 0)),
            whole(covered_rows),
            whole(covered_column),
            chunk,
        ],
        out_specs=chunk,
        scratch_shapes=[
            pltpu.VMEM((pad8(peers * share), LANES), F32),
            pltpu.VMEM(stack.shape, F32),
            pltpu.VMEM((size, wide), BF16),
        ],
        input_output_aliases={3: 0},
        compiler_params=params(12),
        name="body",
    )(replies, covered_rows, covered_column, residual)

    return pl.pallas_call(
        functools.partial(last_kernel, cap),
        grid=(steps,),
        out_shape=out,
        in_specs=[whole(results), whole(slot_column), chunk],
        out_specs=chunk,
        scratch_shapes=[pltpu.VMEM((LANES, LANES), F32), pltpu.VMEM((size, LANES), BF16)],
        input_output_aliases={2: 0},
        compiler_params=params(12),
        name="last",
    )(results, slot_column, residual)


def solution(mesh):
    both = ("px", "py")
    in_specs = (
        P(None, None, both),
        P(None, None, both),
        P(both),
        P(),
        P(),
        P(),
        P(both, None),
        P(both),
        P(both, None, None),
        P(both, None, None),
        P("px"),
        P(both, None, None),
        P(both, None, None),
        P(both, None),
        P(both, None),
    )
    return jax.shard_map(
        local, mesh=mesh, in_specs=in_specs, out_specs=P(None, None, both), check_vma=False
    )
```

profile of v0, /device:TPU:27, one launch (start us, length us, event | category | flops | bytes accessed | tf_op | source)
XLA Modules:
  0.0 76.6 jit_solution(10508456678385813925)
XLA Ops:
  0.0 0.7 copy.18.owner_ref
  0.7 0.0 copy-start.12
  0.7 0.7 copy-done.12
  1.4 0.0 copy-start.13
  1.4 0.7 copy-done.13
  2.2 0.7 copy-done.16
  2.8 0.7 copy-done.18
  3.5 0.7 copy-done.19
  4.2 1.0 %ids.1 = f32[8,8,128]{2,1,0:T(8,128)S(1)} custom-call(s32[6]{0:T(128)S(1)} %copy-done.18, s32[40,1]{1,0:T(8,128)S(1)} %copy.18.owner_ref, s32[1,40]{1,0:T(1,128)S(1)} %bitcast.5, f32[6,3,128]{2,1,0:T(4,128)S(1)} %copy-done.12, f32[6,3,128]{2,1,0:T(4,128)S(1)} %copy-done.13, f32[6,128]{1,0:T(8,128)S(1)} %copy-done.16), custom_call_target="tpu_custom_call" | custom-call | tf_op jit(solution)/shard_map/ids/pallas_call | solution.py:400
  5.2 7.6 %all_to_all.15.got_ref = f32[8,8,128]{2,1,0:T(8,128)S(1)} all-to-all(f32[8,8,128]{2,1,0:T(8,128)S(1)} %ids.1), channel_id=1, replica_groups=mesh['px'=4,'py'=8] {'py'}, dimensions={0} | all-to-all | bytes 65536 | tf_op jit(solution)/shard_map/all_to_all | solution.py:376
  12.8 1.7 %copy-done = f32[5,125,1024]{2,1,0:T(8,128)S(1)} copy-done((f32[5,125,1024]{2,1,0:T(8,128)S(1)}, f32[5,125,1024]{2,1,0:T(8,128)}, u32[]{:S(2)}) %copy-start) | copy-done | bytes 2560024
  14.5 1.7 %copy-done.2 = f32[5,125,1024]{2,1,0:T(8,128)S(1)} copy-done((f32[5,125,1024]{2,1,0:T(8,128)S(1)}, f32[5,125,1024]{2,1,0:T(8,128)}, u32[]{:S(2)}) %copy-start.2) | copy-done | bytes 2560024
  16.3 4.0 %pick.1 = (f32[8,11,8,128]{3,2,1,0:T(8,128)}, s32[128,128]{1,0:T(8,128)S(1)}) custom-call(f32[8,8,128]{2,1,0:T(8,128)S(1)} %all_to_all.15.got_ref, f32[5,125,1024]{2,1,0:T(8,128)S(1)} %copy-done, f32[5,125,1024]{2,1,0:T(8,128)S(1)} %copy-done.2), custom_call_target="tpu_custom_call" | custom-call | tf_op jit(solution)/shard_map/pick/pallas_call | solution.py:428
  20.2 0.6 copy-done.7
  20.9 4.9 %all-to-all-start.1 = ((f32[8,11,8,128]{3,2,1,0:T(8,128)}), f32[8,11,8,128]{3,2,1,0:T(8,128)S(1)}, u32[]{:S(2)}, u32[]{:S(2)}) async-start(f32[8,11,8,128]{3,2,1,0:T(8,128)} %get-tuple-element.11), calls=%async_computation.1 | async-start | bytes 720896 | tf_op jit(solution)/shard_map/all_to_all | solution.py:376
  25.8 0.0 copy-done.1
  25.8 0.0 copy-done.14
  25.8 0.0 copy-start.21
  25.8 2.9 %rim.1 = (f32[5,32,128]{2,1,0:T(8,128)}, f32[5,32,128]{2,1,0:T(8,128)}, f32[5,128,128]{2,1,0:T(8,128)S(1)}, s32[128,128]{1,0:T(8,128)S(1)}) custom-call(f32[5,125,1024]{2,1,0:T(8,128)S(1)} %copy-done.1, s32[6,16]{1,0:T(8,128)S(1)} %copy-done.14), custom_call_target="tpu_custom_call" | custom-call | tf_op jit(solution)/shard_map/rim/pallas_call | solution.py:414
  28.7 1.5 %collective-permute-start = (f32[5,32,128]{2,1,0:T(8,128)}, f32[5,32,128]{2,1,0:T(8,128)S(1)}, u32[]{:S(2)}, u32[]{:S(2)}) collective-permute-start(f32[5,32,128]{2,1,0:T(8,128)} %get-tuple-element.15), channel_id=1, source_target_pairs={{0,8},{8,16},{16,24},{1,9},{9,17},{17,25},{2,10},{10,18},{18,26},{... | collective-permute-start | bytes 245768 | tf_op jit(solution)/shard_map/ppermute | solution.py:372
  30.3 4.6 %collective-permute-start.1 = (f32[5,32,128]{2,1,0:T(8,128)}, f32[5,32,128]{2,1,0:T(8,128)}, u32[]{:S(2)}, u32[]{:S(2)}) collective-permute-start(f32[5,32,128]{2,1,0:T(8,128)} %get-tuple-element.16), channel_id=1, source_target_pairs={{8,0},{16,8},{24,16},{9,1},{17,9},{25,17},{10,2},{18,10},{26,18},{... | collective-permute-start | bytes 245768 | tf_op jit(solution)/shard_map/ppermute | solution.py:372
  34.9 0.0 copy-done.21
  34.9 2.0 %copy.19.mass_ref = f32[40,125,125]{2,1,0:T(8,128)} copy(f32[40,125,125]{2,0,1:T(8,128)S(1)} %copy-done.21) | data formatting | bytes 5000000 | tf_op args[8]
  36.8 0.0 copy-done.22
  36.9 2.0 %copy.20.operator_ref = f32[40,125,125]{2,1,0:T(8,128)} copy(f32[40,125,125]{2,0,1:T(8,128)S(1)} %copy-done.22) | data formatting | bytes 5000000 | tf_op args[9]
  38.8 0.0 copy-done.9
  38.8 0.0 copy-done.23
  38.8 0.6 copy.21.flux_ref
  39.4 0.0 all-to-all-done.1.got_ref
  39.4 0.0 copy-done.17
  39.4 1.7 %copy-done.4 = f32[40,125,125]{2,1,0:T(8,128)S(1)} copy-done((f32[40,125,125]{2,1,0:T(8,128)S(1)}, f32[40,125,125]{2,1,0:T(8,128)}, u32[]{:S(2)}) %copy-start.4) | copy-done | bytes 2500024
  41.2 1.7 %copy-done.5 = f32[40,125,125]{2,1,0:T(8,128)S(1)} copy-done((f32[40,125,125]{2,1,0:T(8,128)S(1)}, f32[40,125,125]{2,1,0:T(8,128)}, u32[]{:S(2)}) %copy-start.5) | copy-done | bytes 2500024
  42.9 5.4 %cut.1 = f32[8,5,8,128]{3,2,1,0:T(8,128)} custom-call(s32[40]{0:T(128)S(1)} %bitcast.4, f32[8,11,8,128]{3,2,1,0:T(8,128)S(1)} %all-to-all-done.1.got_ref, f32[40,125,125]{2,1,0:T(8,128)S(1)} %copy-done.4, f32[40,125,125]{2,1,0:T(8,128)S(1)} %copy-done.5), custom_call_target="tpu_custom_call" | custom-call | tf_op jit(solution)/shard_map/cut/pallas_call | solution.py:477
  48.3 4.8 %all-to-all-start.2 = ((f32[8,5,8,128]{3,2,1,0:T(8,128)}), f32[8,5,8,128]{3,2,1,0:T(8,128)S(1)}, u32[]{:S(2)}, u32[]{:S(2)}) async-start(f32[8,5,8,128]{3,2,1,0:T(8,128)} %cut.1), calls=%async_computation.2 | async-start | bytes 327680 | tf_op jit(solution)/shard_map/all_to_all | solution.py:376
  53.1 0.0 collective-permute-done.below_ref
  53.1 0.0 collective-permute-done.1.above_ref
  53.1 0.0 copy-start.3
  53.1 1.7 %copy-done.3 = f32[5,125,1024]{2,1,0:T(8,128)S(1)} copy-done((f32[5,125,1024]{2,1,0:T(8,128)S(1)}, f32[5,125,1024]{2,1,0:T(8,128)}, u32[]{:S(2)}) %copy-start.3) | copy-done | bytes 2560024
  54.9 0.9 %copy-done.6 = f32[3,125,125]{2,1,0:T(8,128)S(1)} copy-done((f32[3,125,125]{2,1,0:T(8,128)S(1)}, f32[3,125,125]{2,1,0:T(8,128)}, u32[]{:S(2)}) %copy-start.6) | copy-done | bytes 187524
  55.8 0.7 copy-done.11
  56.5 0.7 copy-done.15
  57.2 0.7 copy-done.20
  57.8 7.6 %main.1.base_ref = f32[5,125,1024]{2,1,0:T(8,128)} custom-call(f32[3,5,5]{2,1,0:T(8,128)S(1)} %copy-done.11, f32[5]{0:T(128)S(1)} %copy-done.20, f32[5,125,1024]{2,1,0:T(8,128)S(1)} %copy-done.1, f32[5,125,1024]{2,1,0:T(8,128)S(1)} %copy-done.1, f32[5,125,1024]{2,1,0:T(8,128)S(1)} %copy-done.1, f32[5,125,1024]{2,1,0:T(8,128)S(1)} %copy-done.3, ...), custom_call_target="tpu_custom_call" | custom-call | flops 2516582400 | bytes 10240000 | tf_op jit(solution)/shard_map/main/pallas_call | solution.py:442
  65.4 0.0 copy-done.10
  65.4 6.6 %body.1.base_ref = f32[5,125,1024]{2,1,0:T(8,128)} custom-call(f32[8,11,8,128]{3,2,1,0:T(8,128)S(1)} %all-to-all-done.1.got_ref, f32[5,128,128]{2,1,0:T(8,128)S(1)} %get-tuple-element.13.rows_ref, s32[128,128]{1,0:T(8,128)S(1)} %copy-done.10, f32[5,125,1024]{2,1,0:T(8,128)} %main.1.base_ref), custom_call_target="tpu_custom_call", output_to_operand_aliasing={{}: (3, {})} | custom-call | tf_op jit(solution)/shard_map/body/pallas_call | solution.py:489
  72.0 0.0 all-to-all-done.2.got_ref
  72.0 0.0 copy-done.8
  72.0 4.6 %last.1 = f32[5,125,1024]{2,1,0:T(8,128)} custom-call(f32[8,5,8,128]{3,2,1,0:T(8,128)S(1)} %all-to-all-done.2.got_ref, s32[128,128]{1,0:T(8,128)S(1)} %copy-done.8, f32[5,125,1024]{2,1,0:T(8,128)} %body.1.base_ref), custom_call_target="tpu_custom_call", output_to_operand_aliasing={{}: (2, {})} | custom-call | tf_op jit(solution)/shard_map/last/pallas_call | solution.py:510
  (20 shorter events, 0.0 us)
Async XLA Ops:
  0.7 0.7 copy-start.12
  1.4 0.7 copy-start.13
  2.2 0.7 copy-start.16
  2.8 0.7 copy-start.18
  3.5 0.7 copy-start.19
  12.8 1.7 %copy-start = (f32[5,125,1024]{2,1,0:T(8,128)S(1)}, f32[5,125,1024]{2,1,0:T(8,128)}, u32[]{:S(2)}) copy-start(f32[5,125,1024]{2,1,0:T(8,128)} %over_ref.1) | copy-start | bytes 7680004
  14.5 1.7 %copy-start.2 = (f32[5,125,1024]{2,1,0:T(8,128)S(1)}, f32[5,125,1024]{2,1,0:T(8,128)}, u32[]{:S(2)}) copy-start(f32[5,125,1024]{2,1,0:T(8,128)} %old_ref.3) | copy-start | bytes 7680004
  16.3 9.5 %copy-start.1 = (f32[5,125,1024]{2,1,0:T(8,128)S(1)}, f32[5,125,1024]{2,1,0:T(8,128)}, u32[]{:S(2)}) copy-start(f32[5,125,1024]{2,1,0:T(8,128)} %over_ref.1) | copy-start | bytes 7680004
  16.3 9.5 %copy-start.14 = (s32[6,16]{1,0:T(8,128)S(1)}, s32[6,16]{1,0:T(8,128)}, u32[]{:S(2)}) copy-start(s32[6,16]{1,0:T(8,128)} %covered_ref.1) | copy-start | bytes 1156
  20.2 0.6 copy-start.7
  20.9 18.6 %all-to-all-start.1 = ((f32[8,11,8,128]{3,2,1,0:T(8,128)}), f32[8,11,8,128]{3,2,1,0:T(8,128)S(1)}, u32[]{:S(2)}, u32[]{:S(2)}) async-start(f32[8,11,8,128]{3,2,1,0:T(8,128)} %get-tuple-element.11), calls=%async_computation.1 | async-start | bytes 720896 | tf_op jit(solution)/shard_map/all_to_all | solution.py:376
  25.8 9.1 %copy-start.21 = (f32[40,125,125]{2,0,1:T(8,128)S(1)}, f32[40,125,125]{2,0,1:T(8,128)}, u32[]{:S(2)}) copy-start(f32[40,125,125]{2,0,1:T(8,128)} %param.23) | copy-start | bytes 7500004
  28.7 10.1 %copy-start.9 = (s32[128,128]{1,0:T(8,128)}, s32[128,128]{1,0:T(8,128)S(1)}, u32[]{:S(2)}) copy-start(s32[128,128]{1,0:T(8,128)S(1)} %get-tuple-element.14.column_ref) | copy-start | bytes 196612
  28.7 8.1 %copy-start.22 = (f32[40,125,125]{2,0,1:T(8,128)S(1)}, f32[40,125,125]{2,0,1:T(8,128)}, u32[]{:S(2)}) copy-start(f32[40,125,125]{2,0,1:T(8,128)} %param.24) | copy-start | bytes 7500004
  28.7 24.4 %collective-permute-start = (f32[5,32,128]{2,1,0:T(8,128)}, f32[5,32,128]{2,1,0:T(8,128)S(1)}, u32[]{:S(2)}, u32[]{:S(2)}) collective-permute-start(f32[5,32,128]{2,1,0:T(8,128)} %get-tuple-element.15), channel_id=1, source_target_pairs={{0,8},{8,16},{16,24},{1,9},{9,17},{17,25},{2,10},{10,18},{18,26},{... | collective-permute-start | bytes 245768 | tf_op jit(solution)/shard_map/ppermute | solution.py:372
  30.3 22.8 %collective-permute-start.1 = (f32[5,32,128]{2,1,0:T(8,128)}, f32[5,32,128]{2,1,0:T(8,128)}, u32[]{:S(2)}, u32[]{:S(2)}) collective-permute-start(f32[5,32,128]{2,1,0:T(8,128)} %get-tuple-element.16), channel_id=1, source_target_pairs={{8,0},{16,8},{24,16},{9,1},{17,9},{25,17},{10,2},{18,10},{26,18},{... | collective-permute-start | bytes 245768 | tf_op jit(solution)/shard_map/ppermute | solution.py:372
  36.9 2.0 %copy-start.23 = (f32[3,5,5]{2,0,1:T(4,128)S(1)}, f32[3,5,5]{2,0,1:T(4,128)}, u32[]{:S(2)}) copy-start(f32[3,5,5]{2,0,1:T(4,128)} %param.19) | copy-start | bytes 904
  36.9 2.6 %copy-start.17 = (s32[40,1]{0,1:T(1,128)S(1)}, s32[40,1]{0,1:T(1,128)}, u32[]{:S(2)}) copy-start(s32[40,1]{0,1:T(1,128)} %param.21) | copy-start | bytes 484
  39.4 1.7 %copy-start.4 = (f32[40,125,125]{2,1,0:T(8,128)S(1)}, f32[40,125,125]{2,1,0:T(8,128)}, u32[]{:S(2)}) copy-start(f32[40,125,125]{2,1,0:T(8,128)} %copy.19.mass_ref) | copy-start | bytes 7500004
  41.2 1.7 %copy-start.5 = (f32[40,125,125]{2,1,0:T(8,128)S(1)}, f32[40,125,125]{2,1,0:T(8,128)}, u32[]{:S(2)}) copy-start(f32[40,125,125]{2,1,0:T(8,128)} %copy.20.operator_ref) | copy-start | bytes 7500004
  48.3 23.7 %all-to-all-start.2 = ((f32[8,5,8,128]{3,2,1,0:T(8,128)}), f32[8,5,8,128]{3,2,1,0:T(8,128)S(1)}, u32[]{:S(2)}, u32[]{:S(2)}) async-start(f32[8,5,8,128]{3,2,1,0:T(8,128)} %cut.1), calls=%async_computation.2 | async-start | bytes 327680 | tf_op jit(solution)/shard_map/all_to_all | solution.py:376
  53.1 1.7 %copy-start.3 = (f32[5,125,1024]{2,1,0:T(8,128)S(1)}, f32[5,125,1024]{2,1,0:T(8,128)}, u32[]{:S(2)}) copy-start(f32[5,125,1024]{2,1,0:T(8,128)} %old_ref.3) | copy-start | bytes 7680004
  54.8 0.9 %copy-start.6 = (f32[3,125,125]{2,1,0:T(8,128)S(1)}, f32[3,125,125]{2,1,0:T(8,128)}, u32[]{:S(2)}) copy-start(f32[3,125,125]{2,1,0:T(8,128)} %operator_ref.2) | copy-start | bytes 562504
  55.8 0.7 copy-start.11
  56.5 0.7 copy-start.15
  57.2 0.7 copy-start.20
  57.8 7.6 %copy-start.10 = (s32[128,128]{1,0:T(8,128)S(1)}, s32[128,128]{1,0:T(8,128)}, u32[]{:S(2)}) copy-start(s32[128,128]{1,0:T(8,128)} %copy-done.9) | copy-start | bytes 196612
  65.4 6.6 %copy-start.8 = (s32[128,128]{1,0:T(8,128)S(1)}, s32[128,128]{1,0:T(8,128)}, u32[]{:S(2)}) copy-start(s32[128,128]{1,0:T(8,128)} %copy-done.7) | copy-start | bytes 196612
where the time goes:
time: 77.6 us; the launch traced here: 76.6 us
  Pallas kernels  32.1 us (41%)
  local copies, waits for them, and re-layouts  21 us (27%)
  starting transfers between devices  15.9 us (20%)
  blocking collectives  7.63 us (10%)
    unnamed x52, local copies, waits for them, and re-layouts  21 us
    all_to_all x2, starting transfers between devices, exchange(): return lax.all_to_all(value, 'py', split_axis=0, concat_axis=0, tiled=True)  9.69 us
    all_to_all x1, blocking collectives, exchange(): return lax.all_to_all(value, 'py', split_axis=0, concat_axis=0, tiled=True)  7.63 us
    pallas_call x1, Pallas kernels, local(): pl.pallas_call(main_kernel, grid=(steps,), out_shape=out, in_specs=[smem(...  7.59 us
    pallas_call x1, Pallas kernels, local(): pl.pallas_call(functools.partial(body_kernel, bodies, count, share), grid...  6.57 us
    ppermute x2, starting transfers between devices, shift(): return lax.ppermute(value, axis, pairs)  6.17 us
    pallas_call x1, Pallas kernels, local(): pl.pallas_call(cut_kernel, grid=(cuts // group,), out_shape=terms, in_spe...  5.39 us
    pallas_call x1, Pallas kernels, local(): pl.pallas_call(functools.partial(last_kernel, cap), grid=(steps,), out_sh...  4.63 us
  transfers between devices with their start and end apart: 4, of which 0 were waited for; matrix products, arithmetic and copies ran while one was open for 6% of the time, Pallas kernels for 29%

commit v1 on v0

v1 whole, which is shorter than its diff:
```python
import functools

import jax
import jax.numpy as jnp
from jax import lax
from jax.experimental import pallas as pl
from jax.experimental.pallas import tpu as pltpu
from jax.sharding import PartitionSpec as P

DEGREE = 4
LAYERS = 8
LANES = 128
SUBS = 8
MIB = 1 << 20

F32 = jnp.float32
BF16 = jnp.bfloat16
NN = (((1,), (0,)), ((), ()))
NT = (((1,), (1,)), ((), ()))


def pad8(count):
    return -(-count // SUBS) * SUBS


def iota(shape, dim):
    return lax.broadcasted_iota(jnp.int32, shape, dim)


def halves(value):
    high = value.astype(BF16)
    return high, (value - high.astype(F32)).astype(BF16)


def mxu(left, right, dims=NN):
    return lax.dot_general(left, right, dims, preferred_element_type=F32)


def product(left, right, dims=NN):
    left_high, left_low = left
    right_high, right_low = right
    return mxu(left_high, right_high, dims) + (
        mxu(left_low, right_high, dims) + mxu(left_high, right_low, dims)
    )


def exact_dot(left, right, dims=NN):
    return lax.dot_general(
        left, right, dims, precision=lax.Precision.HIGHEST, preferred_element_type=F32
    )


def pick_lanes(values, lanes):
    return jnp.take_along_axis(values, jnp.broadcast_to(lanes, values.shape), axis=1)


def params(limit):
    return pltpu.CompilerParams(vmem_limit_bytes=limit * MIB)


def kept():
    return pl.BlockSpec(memory_space=pltpu.VMEM)


def scalars():
    return pl.BlockSpec(memory_space=pltpu.SMEM)


def remote():
    return pl.BlockSpec(memory_space=pl.ANY)


def in_hbm(array):
    return pltpu.with_memory_space_constraint(array, pltpu.HBM)


def in_vmem(array):
    return pltpu.with_memory_space_constraint(array, pltpu.VMEM)


def stored(array):
    return pltpu.HBM(array.shape, array.dtype)


def whole(array):
    return pl.BlockSpec(array.shape, lambda *_: (0,) * len(array.shape))


def trace_sums(ref, var, first, width):
    face = ref.shape[1] // (DEGREE + 1)
    part = [ref[var, i * face : (i + 1) * face, first : first + width] for i in range(DEGREE + 1)]
    even, odd = (part[0] + part[2]) + part[4], part[1] + part[3]
    return even + odd, even - odd


def ids_kernel(cap, share, hold_ref, owner_ref, elem_ref, points_ref, normals_ref, weights_ref, out_ref, rows_ref):
    peers = out_ref.shape[0]
    bodies = points_ref.shape[0]
    cuts = owner_ref.shape[1]
    me = lax.axis_index("py")
    owner = owner_ref[...]
    named = (owner == iota((pad8(peers), cuts), 0)).astype(F32)
    earlier = (iota((cuts, cuts), 0) < iota((cuts, cuts), 1)).astype(F32)
    place = jnp.sum(mxu(named, earlier) * named, axis=0, keepdims=True).astype(jnp.int32)
    compact = (owner * cap + place == iota((LANES, cuts), 0)).astype(F32)
    ids = exact_dot(elem_ref[...].astype(F32) + 1.0, compact, NT) - 1.0
    rows_ref[...] = jnp.zeros_like(rows_ref)
    for body in range(bodies):
        mine = hold_ref[body] == me
        rows_ref[body * 7 : body * 7 + 3] = jnp.where(mine, points_ref[body], 0.0)
        rows_ref[body * 7 + 3 : body * 7 + 6] = jnp.where(mine, normals_ref[body], 0.0)
        rows_ref[body * 7 + 6 : body * 7 + 7] = jnp.where(mine, weights_ref[body : body + 1], 0.0)
    for peer in range(peers):
        out_ref[peer] = jnp.zeros((SUBS, LANES), F32)
        out_ref[peer, 0:1] = ids
        out_ref[peer, 1 : 1 + share] = rows_ref[peer * share : (peer + 1) * share]


def load_kernel(covered_ref, state_hbm, state_ref, first_ref, second_ref, rows_ref, column_ref, acc_ref, sems):
    even = lax.axis_index("px") % 2 == 0
    nvar, modes, elems = state_ref.shape
    face = modes // (DEGREE + 1)
    bodies, count = covered_ref.shape
    copies = [pltpu.make_async_copy(state_hbm.at[var], state_ref.at[var], sems.at[var]) for var in range(nvar)]
    for copy in copies:
        copy.start()

    spread = (iota((count, LANES), 1) % count == iota((count, LANES), 0)).astype(F32)
    tiled = exact_dot(covered_ref[...].astype(F32), spread)
    mine = iota((bodies, LANES), 1) // count == iota((bodies, LANES), 0)
    row = jnp.sum(jnp.where(mine, tiled + 1.0, 0.0), axis=0, keepdims=True) - 1.0
    column_ref[...] = jnp.broadcast_to(row, (LANES, LANES)).T.astype(jnp.int32)
    spots = row.astype(jnp.int32)
    acc_ref[...] = jnp.zeros_like(acc_ref)
    first_ref[...] = jnp.zeros_like(first_ref)
    second_ref[...] = jnp.zeros_like(second_ref)
    for var in range(nvar):
        copies[var].wait()
        lower = trace_sums(state_ref, var, 0, LANES)[1]
        upper = trace_sums(state_ref, var, elems - LANES, LANES)[0]
        first_ref[var, :face] = jnp.where(even, upper, lower)
        second_ref[var, :face] = jnp.where(even, lower, upper)
        found = acc_ref[var, :modes]
        for layer in range(elems // LANES):
            lanes = slice(layer * LANES, (layer + 1) * LANES)
            picked = pick_lanes(state_ref[var, :, lanes], spots & (LANES - 1))
            found = jnp.where((spots + LANES) // LANES == layer + 1, picked, found)
        acc_ref[var, :modes] = found
        rows_ref[var] = acc_ref[var].T


def pick_kernel(cap, share, got_ref, state_ref, old_hbm, out_ref, column_ref, old_ref, acc_ref, sems):
    nvar, modes, elems = state_ref.shape
    peers = got_ref.shape[0]
    half = LANES // 2
    copies = [pltpu.make_async_copy(old_hbm.at[var], old_ref.at[var], sems.at[var]) for var in range(nvar)]
    for copy in copies:
        copy.start()
    lane = iota((1, LANES), 1)
    me = lax.axis_index("py")
    row = jnp.zeros((1, LANES), F32) - 1.0
    for peer in range(peers):
        moved = pltpu.roll(got_ref[peer, 0:1], ((peer - me) * cap + LANES) % LANES, 1)
        row = jnp.where(lane // cap == peer, moved, row)
    row = jnp.where(lane < half, row, pltpu.roll(row, half, 1))
    spots = row.astype(jnp.int32)
    acc_ref[...] = jnp.zeros_like(acc_ref)

    def gather(ref, var, wanted):
        found = acc_ref[var, :modes]
        for layer in range(elems // LANES):
            picked = pick_lanes(ref[var, :, layer * LANES : (layer + 1) * LANES], spots & (LANES - 1))
            found = jnp.where(wanted & ((spots + LANES) // LANES == layer + 1), picked, found)
        acc_ref[var, :modes] = found

    for var in range(nvar):
        gather(state_ref, var, lane < half)
    data = got_ref[0]
    for peer in range(1, peers):
        data = data + got_ref[peer]
    for peer in range(peers):
        out_ref[peer, 2 * nvar, :, :] = data
    column = jnp.broadcast_to(row, (LANES, LANES)).T.astype(jnp.int32)
    if cap < SUBS:
        column_ref[...] = jnp.zeros_like(column_ref) - 1
    for peer in range(peers):
        column_ref[peer * SUBS : peer * SUBS + cap] = column[peer * cap : (peer + 1) * cap]
    for var in range(nvar):
        copies[var].wait()
        gather(old_ref, var, lane >= half)
        rows = acc_ref[var].T
        for peer in range(peers):
            for kind in range(2):
                first = kind * half + peer * cap
                if cap < SUBS:
                    out_ref[peer, kind * nvar + var] = jnp.zeros((SUBS, LANES), F32)
                out_ref[peer, kind * nvar + var, :cap] = rows[first : first + cap]


def main_kernel(
    flux_ref, penalty_ref, jac_ref, operator_hbm, state_hbm, old_hbm, _,
    out_ref, _unused, state_ref, old_ref, operator_ref, padded_ref, matrix_ref, right_ref, product_ref, face_ref, sems,
):
    nvar, modes, elems = state_ref.shape
    degree_one = DEGREE + 1
    face = modes // degree_one
    size = nvar * LANES
    width = face_ref.shape[2]
    copies = [
        pltpu.make_async_copy(source, target, sems.at[index])
        for index, (source, target) in enumerate(
            ((operator_hbm, operator_ref), (state_hbm, state_ref), (old_hbm, old_ref))
        )
    ]
    copies[0].start()
    copies[1].start()
    padded_ref[...] = jnp.zeros_like(padded_ref)
    gap = LANES - modes
    for var in range(nvar):
        for place in (0, size):
            last = place + var * LANES + modes
            right_ref[:, last : last + gap] = jnp.zeros((right_ref.shape[0], gap, width), BF16)

    def digits(index):
        high = jnp.floor((index + 0.5) * (1.0 / face))
        return high, index - face * high

    row_high, row_low = digits(iota((LANES, LANES), 0).astype(F32))
    col_high, col_low = digits(iota((LANES, LANES), 1).astype(F32))
    apart = row_high - col_high
    apart = apart - 2.0 * jnp.floor(0.5 * apart)
    inside = iota((LANES, LANES), 0) < modes
    own_face = jnp.where((row_low == col_low) & (apart == 0.0) & inside, 2.0, 0.0)
    own_face = jnp.where(iota((LANES, LANES), 1) < modes, own_face, 0.0)
    copies[0].wait()
    copies[2].start()
    padded_ref[:, :modes, :modes] = operator_ref[...]
    for var in range(nvar):
        for other in range(nvar):
            block = -(flux_ref[var, 0, other] * padded_ref[0])
            for direction in range(1, 3):
                block = block - flux_ref[var, direction, other] * padded_ref[direction]
            if var == other:
                block = block + penalty_ref[var] * own_face
            high, low = halves(block)
            rows = slice(var * LANES, (var + 1) * LANES)
            for place, part in ((0, high), (size, high), (2 * size, low)):
                matrix_ref[rows, place + other * LANES : place + (other + 1) * LANES] = part
    mid = jnp.floor((row_low + 0.5) * (1.0 / degree_one))
    weight = 8.0 / (
        (2.0 * row_high + 1.0) * (2.0 * mid + 1.0) * (2.0 * (row_low - degree_one * mid) + 1.0)
    )
    weight = jnp.concatenate([weight] * (width // LANES), axis=1)[:modes]

    def split(chunk):
        for var in range(nvar):
            high, low = halves(state_ref[var, :, chunk * width : (chunk + 1) * width])
            for place, part in ((0, high), (size, low)):
                right_ref[chunk % 2, place + var * LANES : place + var * LANES + modes] = part

    def multiply(chunk):
        product_ref[chunk % 2] = mxu(matrix_ref[:, : 2 * size], right_ref[chunk % 2]) + mxu(
            matrix_ref[:, 2 * size :], right_ref[chunk % 2, :size]
        )

    copies[1].wait()
    split(0)
    multiply(0)
    split(1)
    copies[2].wait()
    below = [jnp.zeros((face, LANES), F32)] * nvar
    chunks = elems // width
    for chunk in range(chunks):
        first = chunk * width
        lanes = slice(first, first + width)
        if chunk + 1 < chunks:
            multiply(chunk + 1)
        if chunk + 2 < chunks:
            split(chunk + 2)
        scale = weight * jac_ref[:, lanes]
        for var in range(nvar):
            upper, lower = trace_sums(state_ref, var, first, width)
            if chunk + 1 < chunks:
                above = trace_sums(state_ref, var, first + width, LANES)[1]
            else:
                above = jnp.zeros((face, LANES), F32)
            above = jnp.concatenate([lower[:, LANES:], above], axis=1)
            under = jnp.concatenate([below[var], upper[:, : width - LANES]], axis=1)
            below[var] = upper[:, width - LANES :]
            plus = penalty_ref[var] * (above + under)
            minus = penalty_ref[var] * (above - under)
            for i in range(degree_one):
                face_ref[var, i * face : (i + 1) * face] = minus if i % 2 else plus
            change = state_ref[var, :, lanes] - old_ref[var, :, lanes]
            out_ref[var, :, lanes] = (
                product_ref[chunk % 2, var * LANES : var * LANES + modes] + scale * change
            ) - face_ref[var, :modes]


def cut_kernel(owner_ref, got_ref, mass_hbm, operator_hbm, _, out_ref, mass_ref, operator_ref, left_ref, term_ref, spot_ref, seen_ref, sems):
    groups, modes = mass_ref.shape[:2]
    peers, nvar = out_ref.shape[0], out_ref.shape[1]
    kinds = got_ref.shape[1]
    copies = []
    for group in range(groups):
        rows = slice(group * SUBS, (group + 1) * SUBS)
        copies.append(
            (
                pltpu.make_async_copy(mass_hbm.at[:, rows], mass_ref.at[group], sems.at[0, group]),
                pltpu.make_async_copy(operator_hbm.at[:, rows], operator_ref.at[group], sems.at[1, group]),
            )
        )
        for copy in copies[-1]:
            copy.start()
    out_ref[...] = jnp.zeros_like(out_ref)
    for peer in range(peers):
        seen_ref[peer] = 0
    got = got_ref.reshape(peers * kinds * SUBS, LANES)
    out = out_ref.reshape(peers * nvar * SUBS, LANES)
    for index in range(groups * SUBS):
        owner = owner_ref[index]
        place = seen_ref[owner]
        seen_ref[owner] = place + 1
        spot_ref[index] = owner * (nvar * SUBS) + place
        first = owner * (kinds * SUBS) + place
        states = got[pl.ds(first, nvar, stride=SUBS), :]
        changes = states - got[pl.ds(first + nvar * SUBS, nvar, stride=SUBS), :]
        for kind, value in enumerate((changes, -states)):
            high = value.astype(BF16).astype(F32)
            left_ref[index, 2 * SUBS * kind : 2 * SUBS * kind + nvar] = high
            left_ref[index, 2 * SUBS * kind + SUBS : 2 * SUBS * kind + SUBS + nvar] = value - high
    for group in range(groups):
        for copy in copies[group]:
            copy.wait()
        for inner in range(SUBS):
            index = group * SUBS + inner
            total = None
            for kind, ref in enumerate((mass_ref, operator_ref)):
                block = ref.at[group].reshape(modes * SUBS, modes)[pl.ds(inner, modes, stride=SUBS), :]
                left = left_ref[index, 2 * SUBS * kind : 2 * SUBS * (kind + 1), :modes].astype(BF16)
                for right in halves(block):
                    term = mxu(left, right, NT)
                    total = term if total is None else total + term
            term_ref[index, :, :modes] = total[:SUBS] + total[SUBS:]
    for index in range(groups * SUBS):
        out[pl.ds(spot_ref[index], nvar, stride=SUBS), :modes] = term_ref[index, :nvar, :modes]


def body_kernel(bodies, count, share, got_ref, rows_ref, column_ref, base_ref, out_ref, data_ref, basis_ref, lift_ref, left_ref):
    peers = got_ref.shape[0]
    nvar, modes, elems = out_ref.shape
    degree_one = DEGREE + 1
    for peer in range(peers):
        data_ref[peer * share : (peer + 1) * share] = got_ref[peer, 2 * nvar, 1 : 1 + share]
    lift_ref[...] = jnp.zeros_like(lift_ref)
    mode, degree = iota((LANES, SUBS), 0), iota((LANES, SUBS), 1)
    real = mode < modes
    spreads = []
    for digit in (mode // (degree_one * degree_one), mode // degree_one % degree_one, mode % degree_one):
        chosen = (real & (digit == degree)).astype(BF16)
        spreads.append(jnp.concatenate([chosen, chosen, chosen], axis=1))
    ones = jnp.ones((1, LANES), F32)
    none = jnp.zeros((SUBS - degree_one, LANES), F32)
    for body in range(bodies):
        basis = None
        for axis in range(3):
            coords = data_ref[body * 7 + axis : body * 7 + axis + 1]
            table = [ones, coords]
            for n in range(1, DEGREE):
                table.append(((2.0 * n + 1.0) * coords * table[n] - n * table[n - 1]) / (n + 1.0))
            stacked = jnp.concatenate(table + [none], axis=0)
            high = stacked.astype(BF16)
            middle, low = halves(stacked - high.astype(F32))
            factor = mxu(spreads[axis], jnp.concatenate([high, middle, low], axis=0))
            basis = factor if basis is None else basis * factor
        basis_ref[0, body], basis_ref[1, body] = halves(basis)
    bases = [(basis_ref[0, body], basis_ref[1, body]) for body in range(bodies)]
    traces = []
    for body in range(bodies):
        rows = jnp.concatenate([rows_ref[var, body * count : (body + 1) * count] for var in range(nvar)], axis=0)
        traces.append(product(halves(rows), bases[body]))
    fluxes = []
    for body in range(bodies):
        trace = [traces[body][var * count : (var + 1) * count] for var in range(nvar)]
        normal = [data_ref[body * 7 + 3 + axis : body * 7 + 4 + axis] for axis in range(3)]
        weights = data_ref[body * 7 + 6 : body * 7 + 7]
        speed = normal[0] * trace[1] + normal[1] * trace[2] + normal[2] * trace[3]
        flux = [speed + 0.5 * trace[0]] + [normal[axis] * trace[4] for axis in range(3)] + [1.4 * speed]
        fluxes.append(halves(jnp.concatenate([part * weights for part in flux], axis=0)))
    for body in range(bodies):
        lifted = product(fluxes[body], bases[body], NT)
        for var in range(nvar):
            lift_ref[var, body * count : (body + 1) * count] = lifted[var * count : (var + 1) * count]
    for var in range(nvar):
        high, low = halves(lift_ref[var].T)
        left_ref[var * LANES : (var + 1) * LANES, :LANES] = high
        left_ref[var * LANES : (var + 1) * LANES, LANES:] = low

    width = 2 * LANES
    spots = jnp.concatenate([column_ref[...]] * (width // LANES), axis=1)
    for first in range(0, elems, width):
        chosen = (spots == iota((LANES, width), 1) + first).astype(BF16)
        added = mxu(left_ref[...], jnp.concatenate([chosen, chosen], axis=0))
        for var in range(nvar):
            lanes = slice(first, first + width)
            out_ref[var, :, lanes] = base_ref[var, :, lanes] - added[var * LANES : var * LANES + modes]


def last_kernel(penalty_ref, got_ref, column_ref, first_ref, second_ref, base_ref, out_hbm, out_ref, left_ref, face_ref, sems):
    nvar, modes, elems = out_ref.shape
    slots = column_ref.shape[0]
    degree_one = DEGREE + 1
    face = modes // degree_one
    width = 2 * LANES
    even = lax.axis_index("px") % 2 == 0
    for var in range(nvar):
        rows = got_ref[:, var].reshape(slots, LANES).T
        left_ref[var * LANES : (var + 1) * LANES] = jnp.concatenate(halves(rows), axis=1)
        first, second = first_ref[var, :face], second_ref[var, :face]
        above = penalty_ref[var] * jnp.where(even, first, second)
        below = penalty_ref[var] * jnp.where(even, second, first)
        for i in range(degree_one):
            face_ref[0, var, i * face : (i + 1) * face] = -below if i % 2 else below
            face_ref[1, var, i * face : (i + 1) * face] = above

    spots = jnp.concatenate([column_ref[...]] * (width // LANES), axis=1)
    copies = []
    for start in range(0, elems, width):
        lanes = slice(start, start + width)
        chosen = (spots == iota((slots, width), 1) + start).astype(BF16)
        chosen = jnp.concatenate([chosen, chosen], axis=0)
        for var in range(nvar):
            added = mxu(left_ref[var * LANES : (var + 1) * LANES], chosen)[:modes]
            total = base_ref[var, :, lanes] + added
            if start == 0:
                total = jnp.concatenate([total[:, :LANES] - face_ref[0, var, :modes], total[:, LANES:]], axis=1)
            if start + width == elems:
                total = jnp.concatenate([total[:, :LANES], total[:, LANES:] - face_ref[1, var, :modes]], axis=1)
            out_ref[var, :, lanes] = total
            copies.append(
                pltpu.make_async_copy(out_ref.at[var, :, lanes], out_hbm.at[var, :, lanes], sems.at[len(copies)])
            )
            copies[-1].start()
    for copy in copies:
        copy.wait()


def swap(value, axis, odd):
    count = lax.axis_size(axis)
    pairs = [(low, low + 1) for low in range(odd, count - 1, 2)]
    return lax.ppermute(value, axis, pairs + [(high, low) for low, high in pairs])


def exchange(value):
    return lax.all_to_all(value, "py", split_axis=0, concat_axis=0, tiled=True)


def local(
    current_state, state_old, jacobian, volume_operator_list, flux_jacobian_list, penalty, cut_owner, cut_element,
    cut_mass, cut_operator, body_holder_index, body_points, body_normals, body_weights, covered,
):
    nvar, modes, elems = current_state.shape
    columns = elems // LAYERS
    face = modes // (DEGREE + 1)
    peers = lax.axis_size("py")
    cuts = cut_owner.shape[0]
    bodies, count = covered.shape
    cap = max(2, cuts * 3 // (2 * peers) + 1)
    share = -(-bodies * 7 // peers)
    half = LANES // 2
    slots = peers * SUBS
    assert columns == LANES and peers * cap <= half and bodies * count <= LANES
    assert cap <= SUBS and 1 + share <= SUBS and modes <= LANES and cuts % SUBS == 0
    shaped = jax.ShapeDtypeStruct
    wide = 2 * LANES
    size = nvar * LANES

    owner_row = in_hbm(cut_owner.reshape(1, cuts))
    small = [in_hbm(array) for array in (cut_element.reshape(1, cuts), body_points, body_normals, body_weights)]
    asked = shaped((peers, SUBS, LANES), F32)
    asked = pl.pallas_call(
        functools.partial(ids_kernel, cap, share),
        grid=(1,),
        out_shape=asked,
        in_specs=[scalars(), whole(owner_row)] + [whole(array) for array in small],
        out_specs=whole(asked),
        scratch_shapes=[pltpu.VMEM((pad8(peers * share), LANES), F32)],
        compiler_params=params(4),
        name="ids",
    )(in_hbm(body_holder_index), owner_row, *small)
    requests = exchange(asked)

    field = pltpu.VMEM(current_state.shape, F32)
    face_rows = shaped((nvar, pad8(face), LANES), F32)
    stack = shaped((nvar, LANES, LANES), F32)
    square = shaped((LANES, LANES), jnp.int32)
    scratch = pltpu.VMEM(stack.shape, F32)
    state, first_rim, second_rim, covered_rows, covered_column = pl.pallas_call(
        load_kernel,
        grid=(1,),
        out_shape=(field, face_rows, stored(face_rows), stored(stack), stored(square)),
        in_specs=[whole(covered), remote()],
        out_specs=(kept(), whole(face_rows), whole(face_rows), whole(stack), whole(square)),
        scratch_shapes=[scratch, pltpu.SemaphoreType.DMA((nvar,))],
        compiler_params=params(4),
        name="load",
    )(in_hbm(covered), in_hbm(current_state))
    first_rim = swap(first_rim, "px", 0)

    reply = shaped((peers, 2 * nvar + 1, SUBS, LANES), F32)
    column = shaped((slots, LANES), jnp.int32)
    states_out, slot_column = pl.pallas_call(
        functools.partial(pick_kernel, cap, share),
        grid=(1,),
        out_shape=(reply, stored(column)),
        in_specs=[kept(), kept(), remote()],
        out_specs=(whole(reply), whole(column)),
        scratch_shapes=[pltpu.VMEM(current_state.shape, F32), scratch, pltpu.SemaphoreType.DMA((nvar,))],
        compiler_params=params(6),
        name="pick",
    )(requests, in_vmem(state), in_hbm(state_old))
    replies = exchange(states_out)

    jacobian_row = in_hbm(jacobian.reshape(1, elems))
    residual, second_rim = pl.pallas_call(
        main_kernel,
        grid=(1,),
        out_shape=(field, stored(face_rows)),
        in_specs=[scalars(), scalars(), whole(jacobian_row)] + [remote()] * 4,
        out_specs=(kept(), remote()),
        scratch_shapes=[
            pltpu.VMEM(current_state.shape, F32),
            pltpu.VMEM(current_state.shape, F32),
            pltpu.VMEM(volume_operator_list.shape, F32),
            pltpu.VMEM((3, LANES, LANES), F32),
            pltpu.VMEM((size, 3 * size), BF16),
            pltpu.VMEM((2, 2 * size, wide), BF16),
            pltpu.VMEM((2, size, wide), F32),
            pltpu.VMEM((nvar, LANES, wide), F32),
            pltpu.SemaphoreType.DMA((3,)),
        ],
        input_output_aliases={6: 1},
        compiler_params=params(20),
        cost_estimate=pl.CostEstimate(
            flops=6 * size * size * elems, transcendentals=0, bytes_accessed=4 * 4 * nvar * modes * elems
        ),
        name="main",
    )(
        in_hbm(flux_jacobian_list.transpose(1, 0, 2)), in_hbm(penalty), jacobian_row,
        in_hbm(volume_operator_list), in_hbm(current_state), in_hbm(state_old), in_hbm(second_rim),
    )
    after_main = second_rim
    second_rim = swap(second_rim, "px", 1)

    terms = shaped((peers, nvar, SUBS, LANES), F32)
    groups = cuts // SUBS
    blocks = pltpu.VMEM((groups, modes, SUBS, modes), F32)
    results_out = pl.pallas_call(
        cut_kernel,
        grid=(1,),
        out_shape=terms,
        in_specs=[scalars(), kept(), remote(), remote(), remote()],
        out_specs=whole(terms),
        scratch_shapes=[
            blocks,
            blocks,
            pltpu.VMEM((cuts, 4 * SUBS, LANES), F32),
            pltpu.VMEM((cuts, SUBS, LANES), F32),
            pltpu.SMEM((cuts,), jnp.int32),
            pltpu.SMEM((peers,), jnp.int32),
            pltpu.SemaphoreType.DMA((2, groups)),
        ],
        compiler_params=params(10),
        name="cut",
    )(
        in_hbm(cut_owner.reshape(cuts)), replies,
        in_hbm(cut_mass.transpose(1, 0, 2)), in_hbm(cut_operator.transpose(1, 0, 2)), in_hbm(after_main),
    )
    results = exchange(results_out)

    residual = pl.pallas_call(
        functools.partial(body_kernel, bodies, count, share),
        grid=(1,),
        out_shape=field,
        in_specs=[kept(), whole(stack), whole(square), kept()],
        out_specs=kept(),
        scratch_shapes=[
            pltpu.VMEM((pad8(peers * share), LANES), F32),
            pltpu.VMEM((2, bodies, LANES, LANES), BF16),
            scratch,
            pltpu.VMEM((size, wide), BF16),
        ],
        input_output_aliases={3: 0},
        compiler_params=params(6),
        name="body",
    )(replies, in_hbm(covered_rows), in_hbm(covered_column), in_vmem(residual))

    return pl.pallas_call(
        last_kernel,
        grid=(1,),
        out_shape=shaped(current_state.shape, F32),
        in_specs=[scalars(), kept(), whole(column), kept(), kept(), kept()],
        out_specs=remote(),
        scratch_shapes=[
            pltpu.VMEM(current_state.shape, F32),
            pltpu.VMEM((size, 2 * slots), BF16),
            pltpu.VMEM((2, nvar, LANES, LANES), F32),
            pltpu.SemaphoreType.DMA((nvar * (elems // wide),)),
        ],
        compiler_params=params(8),
        name="last",
    )(in_hbm(penalty), results, in_hbm(slot_column), first_rim, second_rim, in_vmem(residual))


def solution(mesh):
    both = ("px", "py")
    in_specs = (
        P(None, None, both),
        P(None, None, both),
        P(both),
        P(),
        P(),
        P(),
        P(both, None),
        P(both),
        P(both, None, None),
        P(both, None, None),
        P("px"),
        P(both, None, None),
        P(both, None, None),
        P(both, None),
        P(both, None),
    )
    return jax.shard_map(
        local, mesh=mesh, in_specs=in_specs, out_specs=P(None, None, both), check_vma=False
    )
```

time: 77.6 us -> 47.1 us (0.61)
  the two profiles are of different devices: /device:TPU:27 before, /device:TPU:18 now
where the time goes in v1:
time: 47.1 us; the launch traced here: 46.4 us
  Pallas kernels  28.2 us (60%)
  starting transfers between devices  16.2 us (34%)
  waiting for transfers between devices  1.88 us (4%)
    all_to_all x3, starting transfers between devices, exchange(): return lax.all_to_all(value, 'py', split_axis=0, concat_axis=0, tiled=True)  12.7 us
    pallas_call x1, Pallas kernels, local(): pl.pallas_call(main_kernel, grid=(1,), out_shape=(field, stored(face_rows...  7.45 us
    pallas_call x1, Pallas kernels, local(): pl.pallas_call(cut_kernel, grid=(1,), out_shape=terms, in_specs=[scalars(...  6.11 us
    pallas_call x1, Pallas kernels, local(): pl.pallas_call(load_kernel, grid=(1,), out_shape=(field, face_rows, store...  3.94 us
    pallas_call x1, Pallas kernels, local(): pl.pallas_call(functools.partial(pick_kernel, cap, share), grid=(1,), out...  3.58 us
    ppermute x2, starting transfers between devices, swap(): lax.ppermute(value, axis, pairs + [(high, low) for low, high in pairs])  3.49 us
    pallas_call x1, Pallas kernels, local(): pl.pallas_call(last_kernel, grid=(1,), out_shape=shaped(current_state.sha...  2.82 us
    pallas_call x1, Pallas kernels, local(): pl.pallas_call(functools.partial(body_kernel, bodies, count, share), grid...  2.52 us
  transfers between devices with their start and end apart: 5, of which 1 were waited for; matrix products, arithmetic and copies ran while one was open for 0% of the time, Pallas kernels for 30%

profile of v1, /device:TPU:18, one launch (start us, length us, event | category | flops | bytes accessed | tf_op | source)
XLA Modules:
  0.0 46.4 jit_solution(5815467285039927196)
XLA Ops:
  0.0 1.8 %ids.1 = f32[8,8,128]{2,1,0:T(8,128)} custom-call(s32[6]{0:T(128)} %hold_ref.1, s32[1,40]{1,0:T(1,128)} %bitcast.9, s32[1,40]{1,0:T(1,128)} %bitcast.11, f32[6,3,128]{2,1,0:T(4,128)} %points_ref.1, f32[6,3,128]{2,1,0:T(4,128)} %normals_ref.1, f32[6,128]{1,0:T(8,128)} %weights_ref.1), custom_call_target="tpu_custom_call" | custom-call | tf_op jit(solution)/shard_map/ids/pallas_call | solution.py:481
  1.8 4.3 %all-to-all-start = ((f32[8,8,128]{2,1,0:T(8,128)}), f32[8,8,128]{2,1,0:T(8,128)S(1)}, u32[]{:S(2)}, u32[]{:S(2)}) async-start(f32[8,8,128]{2,1,0:T(8,128)} %ids.1), calls=%async_computation | async-start | bytes 65536 | tf_op jit(solution)/shard_map/all_to_all | solution.py:455
  6.0 3.9 %load.1 = (f32[5,125,1024]{2,1,0:T(8,128)S(1)}, f32[5,32,128]{2,1,0:T(8,128)S(1)}, f32[5,32,128]{2,1,0:T(8,128)}, f32[5,128,128]{2,1,0:T(8,128)}, s32[128,128]{1,0:T(8,128)}) custom-call(s32[6,16]{1,0:T(8,128)} %covered_ref.1, f32[5,125,1024]{2,1,0:T(8,128)} %state_hbm.3), custom_call_target="tpu_custom_call" | custom-call | tf_op jit(solution)/shard_map/load/pallas_call | solution.py:498
  10.0 0.0 all-to-all-done.got_ref
  10.0 3.6 %pick.1 = (f32[8,11,8,128]{3,2,1,0:T(8,128)}, s32[64,128]{1,0:T(8,128)}) custom-call(f32[8,8,128]{2,1,0:T(8,128)S(1)} %all-to-all-done.got_ref, f32[5,125,1024]{2,1,0:T(8,128)S(1)} %get-tuple-element.14.state_ref, f32[5,125,1024]{2,1,0:T(8,128)} %old_hbm.3), custom_call_target="tpu_custom_call" | custom-call | tf_op jit(solution)/shard_map/pick/pallas_call | solution.py:512
  13.6 4.2 %all-to-all-start.1 = ((f32[8,11,8,128]{3,2,1,0:T(8,128)}), f32[8,11,8,128]{3,2,1,0:T(8,128)S(1)}, u32[]{:S(2)}, u32[]{:S(2)}) async-start(f32[8,11,8,128]{3,2,1,0:T(8,128)} %get-tuple-element.15), calls=%async_computation.1 | async-start | bytes 720896 | tf_op jit(solution)/shard_map/all_to_all | solution.py:455
  17.8 7.5 %main.1 = (f32[5,125,1024]{2,1,0:T(8,128)S(1)}, f32[5,32,128]{2,1,0:T(8,128)}) custom-call(f32[5,3,5]{2,1,0:T(4,128)} %bitcast.12, f32[5]{0:T(128)} %penalty_ref.3, f32[1,1024]{1,0:T(1,128)} %bitcast.13, f32[3,125,125]{2,1,0:T(8,128)} %operator_hbm.1, f32[5,125,1024]{2,1,0:T(8,128)} %state_hbm.3, ...), custom_call_target="tpu_custom_call", output_to_operand_aliasing={{1}: (6, {})} | custom-call | flops 2516582400 | bytes 10240000 | tf_op jit(solution)/shard_map/main/pallas_call | solution.py:525
  25.3 0.0 all-to-all-done.1.got_ref
  25.3 0.0 copy-start
  25.3 6.1 %cut.1 = f32[8,5,8,128]{3,2,1,0:T(8,128)} custom-call(s32[40]{0:T(128)} %bitcast.10, f32[8,11,8,128]{3,2,1,0:T(8,128)S(1)} %all-to-all-done.1.got_ref, f32[125,40,125]{2,1,0:T(8,128)} %bitcast.7, f32[125,40,125]{2,1,0:T(8,128)} %bitcast.8, f32[5,32,128]{2,1,0:T(8,128)} %get-tuple-element.17._), custom_call_target="tpu_custom_call" | custom-call | tf_op jit(solution)/shard_map/cut/pallas_call | solution.py:558
  31.4 4.2 %all-to-all-start.2 = ((f32[8,5,8,128]{3,2,1,0:T(8,128)}), f32[8,5,8,128]{3,2,1,0:T(8,128)S(1)}, u32[]{:S(2)}, u32[]{:S(2)}) async-start(f32[8,5,8,128]{3,2,1,0:T(8,128)} %cut.1), calls=%async_computation.2 | async-start | bytes 327680 | tf_op jit(solution)/shard_map/all_to_all | solution.py:455
  35.7 1.6 %collective-permute-start = (f32[5,32,128]{2,1,0:T(8,128)S(1)}, f32[5,32,128]{2,1,0:T(8,128)S(1)}, u32[]{:S(2)}, u32[]{:S(2)}) collective-permute-start(f32[5,32,128]{2,1,0:T(8,128)S(1)} %get-tuple-element.19), channel_id=1, source_target_pairs={{0,8},{16,24},{8,0},{24,16},{1,9},{17,25},{9,1},{25,17},{2,10},{18... | collective-permute-start | bytes 245768 | tf_op jit(solution)/shard_map/ppermute | solution.py:451
  37.2 0.0 copy-done
  37.2 1.9 %collective-permute-start.1 = (f32[5,32,128]{2,1,0:T(8,128)S(1)}, f32[5,32,128]{2,1,0:T(8,128)S(1)}, u32[]{:S(2)}, u32[]{:S(2)}) collective-permute-start(f32[5,32,128]{2,1,0:T(8,128)S(1)} %copy-done), channel_id=1, source_target_pairs={{8,16},{16,8},{9,17},{17,9},{10,18},{18,10},{11,19},{19,11},{12,20... | collective-permute-start | bytes 245768 | tf_op jit(solution)/shard_map/ppermute | solution.py:451
  39.2 2.5 %body.1.base_ref = f32[5,125,1024]{2,1,0:T(8,128)S(1)} custom-call(f32[8,11,8,128]{3,2,1,0:T(8,128)S(1)} %all-to-all-done.1.got_ref, f32[5,128,128]{2,1,0:T(8,128)} %get-tuple-element.20.rows_ref, s32[128,128]{1,0:T(8,128)} %get-tuple-element.21.column_ref, f32[5,125,1024]{2,1,0:T(8,128)S(1)} %get-tuple-element.22.base_ref), custom_call_target="tpu_custom_call", output_to_operand_aliasing={{}: (3, {})} | custom-call | tf_op jit(solution)/shard_map/body/pallas_call | solution.py:581
  41.7 0.0 collective-permute-done.first_ref
  41.7 1.9 %collective-permute-done.1.second_ref = f32[5,32,128]{2,1,0:T(8,128)S(1)} collective-permute-done((f32[5,32,128]{2,1,0:T(8,128)S(1)}, f32[5,32,128]{2,1,0:T(8,128)S(1)}, u32[]{:S(2)}, u32[]{:S(2)}) %collective-permute-start.1) | collective-permute-done | bytes 81952 | tf_op jit(solution)/shard_map/ppermute | solution.py:451
  43.6 0.0 all-to-all-done.2.got_ref
  43.6 2.8 %last.1 = f32[5,125,1024]{2,1,0:T(8,128)} custom-call(f32[5]{0:T(128)} %penalty_ref.3, f32[8,5,8,128]{3,2,1,0:T(8,128)S(1)} %all-to-all-done.2.got_ref, s32[64,128]{1,0:T(8,128)} %get-tuple-element.18.column_ref, f32[5,32,128]{2,1,0:T(8,128)S(1)} %collective-permute-done.first_ref, f32[5,32,128]{2,1,0:T(8,128)S(1)} %collective-permute-done.1.second_ref, ...), custom_call_target="tpu_custom_call" | custom-call | tf_op jit(solution)/shard_map/last/pallas_call | solution.py:598
Async XLA Ops:
  1.8 8.2 %all-to-all-start = ((f32[8,8,128]{2,1,0:T(8,128)}), f32[8,8,128]{2,1,0:T(8,128)S(1)}, u32[]{:S(2)}, u32[]{:S(2)}) async-start(f32[8,8,128]{2,1,0:T(8,128)} %ids.1), calls=%async_computation | async-start | bytes 65536 | tf_op jit(solution)/shard_map/all_to_all | solution.py:455
  13.6 11.7 %all-to-all-start.1 = ((f32[8,11,8,128]{3,2,1,0:T(8,128)}), f32[8,11,8,128]{3,2,1,0:T(8,128)S(1)}, u32[]{:S(2)}, u32[]{:S(2)}) async-start(f32[8,11,8,128]{3,2,1,0:T(8,128)} %get-tuple-element.15), calls=%async_computation.1 | async-start | bytes 720896 | tf_op jit(solution)/shard_map/all_to_all | solution.py:455
  25.3 11.9 %copy-start = (f32[5,32,128]{2,1,0:T(8,128)S(1)}, f32[5,32,128]{2,1,0:T(8,128)}, u32[]{:S(2)}) copy-start(f32[5,32,128]{2,1,0:T(8,128)} %get-tuple-element.17._) | copy-start | bytes 245764
  31.4 12.1 %all-to-all-start.2 = ((f32[8,5,8,128]{3,2,1,0:T(8,128)}), f32[8,5,8,128]{3,2,1,0:T(8,128)S(1)}, u32[]{:S(2)}, u32[]{:S(2)}) async-start(f32[8,5,8,128]{3,2,1,0:T(8,128)} %cut.1), calls=%async_computation.2 | async-start | bytes 327680 | tf_op jit(solution)/shard_map/all_to_all | solution.py:455
  35.7 6.0 %collective-permute-start = (f32[5,32,128]{2,1,0:T(8,128)S(1)}, f32[5,32,128]{2,1,0:T(8,128)S(1)}, u32[]{:S(2)}, u32[]{:S(2)}) collective-permute-start(f32[5,32,128]{2,1,0:T(8,128)S(1)} %get-tuple-element.19), channel_id=1, source_target_pairs={{0,8},{16,24},{8,0},{24,16},{1,9},{17,25},{9,1},{25,17},{2,10},{18... | collective-permute-start | bytes 245768 | tf_op jit(solution)/shard_map/ppermute | solution.py:451
  37.2 6.3 %collective-permute-start.1 = (f32[5,32,128]{2,1,0:T(8,128)S(1)}, f32[5,32,128]{2,1,0:T(8,128)S(1)}, u32[]{:S(2)}, u32[]{:S(2)}) collective-permute-start(f32[5,32,128]{2,1,0:T(8,128)S(1)} %copy-done), channel_id=1, source_target_pairs={{8,16},{16,8},{9,17},{17,9},{10,18},{18,10},{11,19},{19,11},{12,20... | collective-permute-start | bytes 245768 | tf_op jit(solution)/shard_map/ppermute | solution.py:451

commit v2 on v1

--- a/solution.py
+++ b/solution.py
@@ -116,14 +116,22 @@
         out_ref[peer, 1 : 1 + share] = rows_ref[peer * share : (peer + 1) * share]
 
 
-def load_kernel(covered_ref, state_hbm, state_ref, first_ref, second_ref, rows_ref, column_ref, acc_ref, sems):
+def load_kernel(
+    covered_hbm, state_hbm, state_ref, first_ref, second_ref, rows_ref, column_ref, covered_ref, acc_ref, sems
+):
     even = lax.axis_index("px") % 2 == 0
     nvar, modes, elems = state_ref.shape
     face = modes // (DEGREE + 1)
     bodies, count = covered_ref.shape
     copies = [pltpu.make_async_copy(state_hbm.at[var], state_ref.at[var], sems.at[var]) for var in range(nvar)]
+    covered_copy = pltpu.make_async_copy(covered_hbm, covered_ref, sems.at[nvar])
+    covered_copy.start()
     for copy in copies:
         copy.start()
+    acc_ref[...] = jnp.zeros_like(acc_ref)
+    first_ref[...] = jnp.zeros_like(first_ref)
+    second_ref[...] = jnp.zeros_like(second_ref)
+    covered_copy.wait()
 
     spread = (iota((count, LANES), 1) % count == iota((count, LANES), 0)).astype(F32)
     tiled = exact_dot(covered_ref[...].astype(F32), spread)
@@ -131,9 +139,6 @@
     row = jnp.sum(jnp.where(mine, tiled + 1.0, 0.0), axis=0, keepdims=True) - 1.0
     column_ref[...] = jnp.broadcast_to(row, (LANES, LANES)).T.astype(jnp.int32)
     spots = row.astype(jnp.int32)
-    acc_ref[...] = jnp.zeros_like(acc_ref)
-    first_ref[...] = jnp.zeros_like(first_ref)
-    second_ref[...] = jnp.zeros_like(second_ref)
     for var in range(nvar):
         copies[var].wait()
         lower = trace_sums(state_ref, var, 0, LANES)[1]
@@ -198,8 +203,8 @@
 
 
 def main_kernel(
-    flux_ref, penalty_ref, jac_ref, operator_hbm, state_hbm, old_hbm, _,
-    out_ref, _unused, state_ref, old_ref, operator_ref, padded_ref, matrix_ref, right_ref, product_ref, face_ref, sems,
+    flux_hbm, penalty_hbm, jac_hbm, operator_hbm, state_hbm, old_hbm, _,
+    out_ref, _unused, flux_ref, penalty_ref, jac_ref, state_ref, old_ref, operator_ref, padded_ref, matrix_ref, right_ref, product_ref, face_ref, sems,
 ):
     nvar, modes, elems = state_ref.shape
     degree_one = DEGREE + 1
@@ -209,11 +214,18 @@
     copies = [
         pltpu.make_async_copy(source, target, sems.at[index])
         for index, (source, target) in enumerate(
-            ((operator_hbm, operator_ref), (state_hbm, state_ref), (old_hbm, old_ref))
+            (
+                (operator_hbm, operator_ref),
+                (state_hbm, state_ref),
+                (old_hbm, old_ref),
+                (flux_hbm, flux_ref),
+                (penalty_hbm, penalty_ref),
+                (jac_hbm, jac_ref),
+            )
         )
     ]
-    copies[0].start()
-    copies[1].start()
+    for index in (3, 4, 0, 1, 5):
+        copies[index].start()
     padded_ref[...] = jnp.zeros_like(padded_ref)
     gap = LANES - modes
     for var in range(nvar):
@@ -232,7 +244,8 @@
     inside = iota((LANES, LANES), 0) < modes
     own_face = jnp.where((row_low == col_low) & (apart == 0.0) & inside, 2.0, 0.0)
     own_face = jnp.where(iota((LANES, LANES), 1) < modes, own_face, 0.0)
-    copies[0].wait()
+    for index in (3, 4, 0):
+        copies[index].wait()
     copies[2].start()
     padded_ref[:, :modes, :modes] = operator_ref[...]
     for var in range(nvar):
@@ -267,6 +280,7 @@
     split(0)
     multiply(0)
     split(1)
+    copies[5].wait()
     copies[2].wait()
     below = [jnp.zeros((face, LANES), F32)] * nvar
     chunks = elems // width
@@ -297,10 +311,15 @@
             ) - face_ref[var, :modes]
 
 
-def cut_kernel(owner_ref, got_ref, mass_hbm, operator_hbm, _, out_ref, mass_ref, operator_ref, left_ref, term_ref, spot_ref, seen_ref, sems):
+def cut_kernel(
+    owner_hbm, got_ref, mass_hbm, operator_hbm, _, out_ref, owner_ref, mass_ref, operator_ref, left_ref, term_ref,
+    spot_ref, seen_ref, sems,
+):
     groups, modes = mass_ref.shape[:2]
     peers, nvar = out_ref.shape[0], out_ref.shape[1]
     kinds = got_ref.shape[1]
+    owner_copy = pltpu.make_async_copy(owner_hbm, owner_ref, sems.at[0, groups])
+    owner_copy.start()
     copies = []
     for group in range(groups):
         rows = slice(group * SUBS, (group + 1) * SUBS)
@@ -315,6 +334,7 @@
     out_ref[...] = jnp.zeros_like(out_ref)
     for peer in range(peers):
         seen_ref[peer] = 0
+    owner_copy.wait()
     got = got_ref.reshape(peers * kinds * SUBS, LANES)
     out = out_ref.reshape(peers * nvar * SUBS, LANES)
     for index in range(groups * SUBS):
@@ -326,21 +346,23 @@
         states = got[pl.ds(first, nvar, stride=SUBS), :]
         changes = states - got[pl.ds(first + nvar * SUBS, nvar, stride=SUBS), :]
         for kind, value in enumerate((changes, -states)):
+            lanes = slice(kind * LANES, (kind + 1) * LANES)
             high = value.astype(BF16).astype(F32)
-            left_ref[index, 2 * SUBS * kind : 2 * SUBS * kind + nvar] = high
-            left_ref[index, 2 * SUBS * kind + SUBS : 2 * SUBS * kind + SUBS + nvar] = value - high
+            left_ref[index, :nvar, lanes] = high
+            left_ref[index, SUBS : SUBS + nvar, lanes] = value - high
+    zero = jnp.zeros((modes, LANES - modes), F32)
     for group in range(groups):
         for copy in copies[group]:
             copy.wait()
         for inner in range(SUBS):
             index = group * SUBS + inner
-            total = None
-            for kind, ref in enumerate((mass_ref, operator_ref)):
+            blocks = []
+            for ref in (mass_ref, operator_ref):
                 block = ref.at[group].reshape(modes * SUBS, modes)[pl.ds(inner, modes, stride=SUBS), :]
-                left = left_ref[index, 2 * SUBS * kind : 2 * SUBS * (kind + 1), :modes].astype(BF16)
-                for right in halves(block):
-                    term = mxu(left, right, NT)
-                    total = term if total is None else total + term
+                blocks.append(jnp.concatenate([block, zero], axis=1))
+            high, low = halves(jnp.concatenate(blocks, axis=1))
+            left = left_ref[index].astype(BF16)
+            total = mxu(left, high, NT) + mxu(left, low, NT)
             term_ref[index, :, :modes] = total[:SUBS] + total[SUBS:]
     for index in range(groups * SUBS):
         out[pl.ds(spot_ref[index], nvar, stride=SUBS), :modes] = term_ref[index, :nvar, :modes]
@@ -406,37 +428,39 @@
             out_ref[var, :, lanes] = base_ref[var, :, lanes] - added[var * LANES : var * LANES + modes]
 
 
-def last_kernel(penalty_ref, got_ref, column_ref, first_ref, second_ref, base_ref, out_hbm, out_ref, left_ref, face_ref, sems):
+def rim_kernel(penalty_ref, first_ref, second_ref, base_ref, out_ref, face_ref):
     nvar, modes, elems = out_ref.shape
-    slots = column_ref.shape[0]
     degree_one = DEGREE + 1
     face = modes // degree_one
-    width = 2 * LANES
     even = lax.axis_index("px") % 2 == 0
-    for var in range(nvar):
-        rows = got_ref[:, var].reshape(slots, LANES).T
-        left_ref[var * LANES : (var + 1) * LANES] = jnp.concatenate(halves(rows), axis=1)
+    bottom, top = slice(0, LANES), slice(elems - LANES, elems)
+    for var in range(nvar):
         first, second = first_ref[var, :face], second_ref[var, :face]
         above = penalty_ref[var] * jnp.where(even, first, second)
         below = penalty_ref[var] * jnp.where(even, second, first)
         for i in range(degree_one):
             face_ref[0, var, i * face : (i + 1) * face] = -below if i % 2 else below
             face_ref[1, var, i * face : (i + 1) * face] = above
-
+    for var in range(nvar):
+        out_ref[var, :, bottom] = base_ref[var, :, bottom] - face_ref[0, var, :modes]
+        out_ref[var, :, top] = base_ref[var, :, top] - face_ref[1, var, :modes]
+
+
+def last_kernel(got_ref, column_ref, base_ref, out_hbm, out_ref, left_ref, sems):
+    nvar, modes, elems = out_ref.shape
+    slots = column_ref.shape[0]
+    width = 2 * LANES
+    for var in range(nvar):
+        rows = got_ref[:, var].reshape(slots, LANES).T
+        left_ref[var * LANES : (var + 1) * LANES] = jnp.concatenate(halves(rows), axis=1)
     spots = jnp.concatenate([column_ref[...]] * (width // LANES), axis=1)
     copies = []
     for start in range(0, elems, width):
         lanes = slice(start, start + width)
         chosen = (spots == iota((slots, width), 1) + start).astype(BF16)
-        chosen = jnp.concatenate([chosen, chosen], axis=0)
+        added = mxu(left_ref[...], jnp.concatenate([chosen, chosen], axis=0))
         for var in range(nvar):
-            added = mxu(left_ref[var * LANES : (var + 1) * LANES], chosen)[:modes]
-            total = base_ref[var, :, lanes] + added
-            if start == 0:
-                total = jnp.concatenate([total[:, :LANES] - face_ref[0, var, :modes], total[:, LANES:]], axis=1)
-            if start + width == elems:
-                total = jnp.concatenate([total[:, :LANES], total[:, LANES:] - face_ref[1, var, :modes]], axis=1)
-            out_ref[var, :, lanes] = total
+            out_ref[var, :, lanes] = base_ref[var, :, lanes] + added[var * LANES : var * LANES + modes]
             copies.append(
                 pltpu.make_async_copy(out_ref.at[var, :, lanes], out_hbm.at[var, :, lanes], sems.at[len(copies)])
             )
@@ -481,9 +505,9 @@
     asked = pl.pallas_call(
         functools.partial(ids_kernel, cap, share),
         grid=(1,),
-        out_shape=asked,
+        out_shape=pltpu.VMEM(asked.shape, F32),
         in_specs=[scalars(), whole(owner_row)] + [whole(array) for array in small],
-        out_specs=whole(asked),
+        out_specs=kept(),
         scratch_shapes=[pltpu.VMEM((pad8(peers * share), LANES), F32)],
         compiler_params=params(4),
         name="ids",
@@ -499,9 +523,13 @@
         load_kernel,
         grid=(1,),
         out_shape=(field, face_rows, stored(face_rows), stored(stack), stored(square)),
-        in_specs=[whole(covered), remote()],
+        in_specs=[remote(), remote()],
         out_specs=(kept(), whole(face_rows), whole(face_rows), whole(stack), whole(square)),
-        scratch_shapes=[scratch, pltpu.SemaphoreType.DMA((nvar,))],
+        scratch_shapes=[
+            pltpu.VMEM(covered.shape, jnp.int32),
+            scratch,
+            pltpu.SemaphoreType.DMA((nvar + 1,)),
+        ],
         compiler_params=params(4),
         name="load",
     )(in_hbm(covered), in_hbm(current_state))
@@ -512,9 +540,9 @@
     states_out, slot_column = pl.pallas_call(
         functools.partial(pick_kernel, cap, share),
         grid=(1,),
-        out_shape=(reply, stored(column)),
+        out_shape=(pltpu.VMEM(reply.shape, F32), pltpu.VMEM(column.shape, column.dtype)),
         in_specs=[kept(), kept(), remote()],
-        out_specs=(whole(reply), whole(column)),
+        out_specs=(kept(), kept()),
         scratch_shapes=[pltpu.VMEM(current_state.shape, F32), scratch, pltpu.SemaphoreType.DMA((nvar,))],
         compiler_params=params(6),
         name="pick",
@@ -526,9 +554,12 @@
         main_kernel,
         grid=(1,),
         out_shape=(field, stored(face_rows)),
-        in_specs=[scalars(), scalars(), whole(jacobian_row)] + [remote()] * 4,
+        in_specs=[remote()] * 7,
         out_specs=(kept(), remote()),
         scratch_shapes=[
+            pltpu.SMEM((nvar, 3, nvar), F32),
+            pltpu.SMEM((nvar,), F32),
+            pltpu.VMEM((1, elems), F32),
             pltpu.VMEM(current_state.shape, F32),
             pltpu.VMEM(current_state.shape, F32),
             pltpu.VMEM(volume_operator_list.shape, F32),
@@ -537,7 +568,7 @@
             pltpu.VMEM((2, 2 * size, wide), BF16),
             pltpu.VMEM((2, size, wide), F32),
             pltpu.VMEM((nvar, LANES, wide), F32),
-            pltpu.SemaphoreType.DMA((3,)),
+            pltpu.SemaphoreType.DMA((6,)),
         ],
         input_output_aliases={6: 1},
         compiler_params=params(20),
@@ -558,17 +589,18 @@
     results_out = pl.pallas_call(
         cut_kernel,
         grid=(1,),
-        out_shape=terms,
-        in_specs=[scalars(), kept(), remote(), remote(), remote()],
-        out_specs=whole(terms),
+        out_shape=pltpu.VMEM(terms.shape, F32),
+        in_specs=[remote(), kept(), remote(), remote(), remote()],
+        out_specs=kept(),
         scratch_shapes=[
+            pltpu.SMEM((cuts,), jnp.int32),
             blocks,
             blocks,
-            pltpu.VMEM((cuts, 4 * SUBS, LANES), F32),
+            pltpu.VMEM((cuts, 2 * SUBS, 2 * LANES), F32),
             pltpu.VMEM((cuts, SUBS, LANES), F32),
             pltpu.SMEM((cuts,), jnp.int32),
             pltpu.SMEM((peers,), jnp.int32),
-            pltpu.SemaphoreType.DMA((2, groups)),
+            pltpu.SemaphoreType.DMA((2, groups + 1)),
         ],
         compiler_params=params(10),
         name="cut",
@@ -595,21 +627,32 @@
         name="body",
     )(replies, in_hbm(covered_rows), in_hbm(covered_column), in_vmem(residual))
 
+    residual = pl.pallas_call(
+        rim_kernel,
+        grid=(1,),
+        out_shape=field,
+        in_specs=[scalars()] + [kept()] * 3,
+        out_specs=kept(),
+        scratch_shapes=[pltpu.VMEM((2, nvar, LANES, LANES), F32)],
+        input_output_aliases={3: 0},
+        compiler_params=params(2),
+        name="rim",
+    )(in_hbm(penalty), first_rim, second_rim, in_vmem(residual))
+
     return pl.pallas_call(
         last_kernel,
         grid=(1,),
         out_shape=shaped(current_state.shape, F32),
-        in_specs=[scalars(), kept(), whole(column), kept(), kept(), kept()],
+        in_specs=[kept(), kept(), kept()],
         out_specs=remote(),
         scratch_shapes=[
             pltpu.VMEM(current_state.shape, F32),
             pltpu.VMEM((size, 2 * slots), BF16),
-            pltpu.VMEM((2, nvar, LANES, LANES), F32),
             pltpu.SemaphoreType.DMA((nvar * (elems // wide),)),
         ],
         compiler_params=params(8),
         name="last",
-    )(in_hbm(penalty), results, in_hbm(slot_column), first_rim, second_rim, in_vmem(residual))
+    )(results, in_vmem(slot_column), in_vmem(residual))
 
 
 def solution(mesh):

time: 47.1 us -> 44.9 us (0.953)
  Pallas kernels: 28.2 us -> 25.1 us
  starting transfers between devices: 16.2 us -> 17.2 us
    pallas_call x1 -> x2, Pallas kernels: 6.11 us -> 5.13 us  [the longest x1 4.27 us: local(): pl.pallas_call(cut_kernel, grid=(1,), out_shape=pltpu.VMEM(terms.shape, F...]
    all_to_all x3, starting transfers between devices: 12.7 us -> 13.7 us  [exchange(): return lax.all_to_all(value, 'py', split_axis=0, concat_axis=0, tiled=True)]
    pallas_call x1, Pallas kernels: 7.45 us -> 6.65 us  [local(): pl.pallas_call(main_kernel, grid=(1,), out_shape=(field, stored(face_rows...]
    pallas_call x1, Pallas kernels: 3.94 us -> 3.27 us  [local(): pl.pallas_call(load_kernel, grid=(1,), out_shape=(field, face_rows, store...]
    pallas_call x1, Pallas kernels: 2.82 us -> 2.2 us  [local(): pl.pallas_call(last_kernel, grid=(1,), out_shape=shaped(current_state.sha...]
  transfers between devices with their start and end apart: 5 -> 5, of which waited for: 1 -> 2; matrix products, arithmetic and copies ran while one was open for 0% -> 0% of each run, Pallas kernels for 30% -> 30%
where the time goes in v2:
time: 44.9 us; the launch traced here: 44.4 us
  Pallas kernels  25.1 us (56%)
  starting transfers between devices  17.2 us (38%)
  waiting for transfers between devices  1.99 us (4%)
    all_to_all x3, starting transfers between devices, exchange(): return lax.all_to_all(value, 'py', split_axis=0, concat_axis=0, tiled=True)  13.7 us
    pallas_call x1, Pallas kernels, local(): pl.pallas_call(main_kernel, grid=(1,), out_shape=(field, stored(face_rows...  6.65 us
    pallas_call x1, Pallas kernels, local(): pl.pallas_call(cut_kernel, grid=(1,), out_shape=pltpu.VMEM(terms.shape, F...  4.27 us
    pallas_call x1, Pallas kernels, local(): pl.pallas_call(functools.partial(pick_kernel, cap, share), grid=(1,), out...  3.56 us
    ppermute x2, starting transfers between devices, swap(): lax.ppermute(value, axis, pairs + [(high, low) for low, high in pairs])  3.49 us
    pallas_call x1, Pallas kernels, local(): pl.pallas_call(load_kernel, grid=(1,), out_shape=(field, face_rows, store...  3.27 us
    pallas_call x1, Pallas kernels, local(): pl.pallas_call(functools.partial(body_kernel, bodies, count, share), grid...  2.52 us
    pallas_call x1, Pallas kernels, local(): pl.pallas_call(last_kernel, grid=(1,), out_shape=shaped(current_state.sha...  2.2 us
  transfers between devices with their start and end apart: 5, of which 2 were waited for; matrix products, arithmetic and copies ran while one was open for 0% of the time, Pallas kernels for 30%

profile of v2, /device:TPU:18, one launch (start us, length us, event | category | flops | bytes accessed | tf_op | source)
XLA Modules:
  0.0 44.4 jit_solution(7126409012570578418)
XLA Ops:
  0.0 1.8 %ids.1 = f32[8,8,128]{2,1,0:T(8,128)} custom-call(s32[6]{0:T(128)} %hold_ref.1, s32[1,40]{1,0:T(1,128)} %bitcast.9, s32[1,40]{1,0:T(1,128)} %bitcast.11, f32[6,3,128]{2,1,0:T(4,128)} %points_ref.1, f32[6,3,128]{2,1,0:T(4,128)} %normals_ref.1, f32[6,128]{1,0:T(8,128)} %weights_ref.1), custom_call_target="tpu_custom_call" | custom-call | tf_op jit(solution)/shard_map/ids/pallas_call | solution.py:505
  1.8 4.3 %all-to-all-start = ((f32[8,8,128]{2,1,0:T(8,128)}), f32[8,8,128]{2,1,0:T(8,128)S(1)}, u32[]{:S(2)}, u32[]{:S(2)}) async-start(f32[8,8,128]{2,1,0:T(8,128)} %ids.1), calls=%async_computation | async-start | bytes 65536 | tf_op jit(solution)/shard_map/all_to_all | solution.py:479
  6.0 3.3 %load.1 = (f32[5,125,1024]{2,1,0:T(8,128)S(1)}, f32[5,32,128]{2,1,0:T(8,128)S(1)}, f32[5,32,128]{2,1,0:T(8,128)}, f32[5,128,128]{2,1,0:T(8,128)}, s32[128,128]{1,0:T(8,128)}) custom-call(s32[6,16]{1,0:T(8,128)} %covered_hbm.1, f32[5,125,1024]{2,1,0:T(8,128)} %state_hbm.3), custom_call_target="tpu_custom_call" | custom-call | tf_op jit(solution)/shard_map/load/pallas_call | solution.py:522
  9.3 0.1 all-to-all-done.got_ref
  9.4 3.6 %pick.1 = (f32[8,11,8,128]{3,2,1,0:T(8,128)}, s32[64,128]{1,0:T(8,128)S(1)}) custom-call(f32[8,8,128]{2,1,0:T(8,128)S(1)} %all-to-all-done.got_ref, f32[5,125,1024]{2,1,0:T(8,128)S(1)} %get-tuple-element.14.state_ref, f32[5,125,1024]{2,1,0:T(8,128)} %old_hbm.3), custom_call_target="tpu_custom_call" | custom-call | tf_op jit(solution)/shard_map/pick/pallas_call | solution.py:540
  13.0 4.8 %all-to-all-start.1 = ((f32[8,11,8,128]{3,2,1,0:T(8,128)}), f32[8,11,8,128]{3,2,1,0:T(8,128)S(1)}, u32[]{:S(2)}, u32[]{:S(2)}) async-start(f32[8,11,8,128]{3,2,1,0:T(8,128)} %get-tuple-element.15), calls=%async_computation.1 | async-start | bytes 720896 | tf_op jit(solution)/shard_map/all_to_all | solution.py:479
  17.8 6.6 %main.1 = (f32[5,125,1024]{2,1,0:T(8,128)S(1)}, f32[5,32,128]{2,1,0:T(8,128)}) custom-call(f32[5,3,5]{2,1,0:T(4,128)} %bitcast.12, f32[5]{0:T(128)} %penalty_ref.1, f32[1,1024]{1,0:T(1,128)} %bitcast.13, f32[3,125,125]{2,1,0:T(8,128)} %operator_hbm.1, f32[5,125,1024]{2,1,0:T(8,128)} %state_hbm.3, ...), custom_call_target="tpu_custom_call", output_to_operand_aliasing={{1}: (6, {})} | custom-call | flops 2516582400 | bytes 10240000 | tf_op jit(solution)/shard_map/main/pallas_call | solution.py:553
  24.5 0.0 all-to-all-done.1.got_ref
  24.5 0.0 copy-start
  24.5 4.3 %cut.1 = f32[8,5,8,128]{3,2,1,0:T(8,128)} custom-call(s32[40]{0:T(128)} %bitcast.10, f32[8,11,8,128]{3,2,1,0:T(8,128)S(1)} %all-to-all-done.1.got_ref, f32[125,40,125]{2,1,0:T(8,128)} %bitcast.7, f32[125,40,125]{2,1,0:T(8,128)} %bitcast.8, f32[5,32,128]{2,1,0:T(8,128)} %get-tuple-element.17._), custom_call_target="tpu_custom_call" | custom-call | tf_op jit(solution)/shard_map/cut/pallas_call | solution.py:589
  28.8 4.6 %all-to-all-start.2 = ((f32[8,5,8,128]{3,2,1,0:T(8,128)}), f32[8,5,8,128]{3,2,1,0:T(8,128)S(1)}, u32[]{:S(2)}, u32[]{:S(2)}) async-start(f32[8,5,8,128]{3,2,1,0:T(8,128)} %cut.1), calls=%async_computation.2 | async-start | bytes 327680 | tf_op jit(solution)/shard_map/all_to_all | solution.py:479
  33.4 1.6 %collective-permute-start = (f32[5,32,128]{2,1,0:T(8,128)S(1)}, f32[5,32,128]{2,1,0:T(8,128)S(1)}, u32[]{:S(2)}, u32[]{:S(2)}) collective-permute-start(f32[5,32,128]{2,1,0:T(8,128)S(1)} %get-tuple-element.19), channel_id=1, source_target_pairs={{0,8},{16,24},{8,0},{24,16},{1,9},{17,25},{9,1},{25,17},{2,10},{18... | collective-permute-start | bytes 245768 | tf_op jit(solution)/shard_map/ppermute | solution.py:475
  35.0 0.0 copy-done
  35.0 1.9 %collective-permute-start.1 = (f32[5,32,128]{2,1,0:T(8,128)S(1)}, f32[5,32,128]{2,1,0:T(8,128)S(1)}, u32[]{:S(2)}, u32[]{:S(2)}) collective-permute-start(f32[5,32,128]{2,1,0:T(8,128)S(1)} %copy-done), channel_id=1, source_target_pairs={{8,16},{16,8},{9,17},{17,9},{10,18},{18,10},{11,19},{19,11},{12,20... | collective-permute-start | bytes 245768 | tf_op jit(solution)/shard_map/ppermute | solution.py:475
  36.9 2.5 %body.1.base_ref = f32[5,125,1024]{2,1,0:T(8,128)S(1)} custom-call(f32[8,11,8,128]{3,2,1,0:T(8,128)S(1)} %all-to-all-done.1.got_ref, f32[5,128,128]{2,1,0:T(8,128)} %get-tuple-element.20.rows_ref, s32[128,128]{1,0:T(8,128)} %get-tuple-element.21.column_ref, f32[5,125,1024]{2,1,0:T(8,128)S(1)} %get-tuple-element.22.base_ref), custom_call_target="tpu_custom_call", output_to_operand_aliasing={{}: (3, {})} | custom-call | tf_op jit(solution)/shard_map/body/pallas_call | solution.py:613
  39.4 0.0 collective-permute-done.first_ref
  39.4 1.9 %collective-permute-done.1.second_ref = f32[5,32,128]{2,1,0:T(8,128)S(1)} collective-permute-done((f32[5,32,128]{2,1,0:T(8,128)S(1)}, f32[5,32,128]{2,1,0:T(8,128)S(1)}, u32[]{:S(2)}, u32[]{:S(2)}) %collective-permute-start.1) | collective-permute-done | bytes 81952 | tf_op jit(solution)/shard_map/ppermute | solution.py:475
  41.3 0.9 %rim.1.base_ref = f32[5,125,1024]{2,1,0:T(8,128)S(1)} custom-call(f32[5]{0:T(128)} %penalty_ref.1, f32[5,32,128]{2,1,0:T(8,128)S(1)} %collective-permute-done.first_ref, f32[5,32,128]{2,1,0:T(8,128)S(1)} %collective-permute-done.1.second_ref, f32[5,125,1024]{2,1,0:T(8,128)S(1)} %body.1.base_ref), custom_call_target="tpu_custom_call", output_to_operand_aliasing={{}: (3, {})} | custom-call | tf_op jit(solution)/shard_map/rim/pallas_call | solution.py:630
  42.2 0.0 all-to-all-done.2.got_ref
  42.2 2.2 %last.1 = f32[5,125,1024]{2,1,0:T(8,128)} custom-call(f32[8,5,8,128]{3,2,1,0:T(8,128)S(1)} %all-to-all-done.2.got_ref, s32[64,128]{1,0:T(8,128)S(1)} %get-tuple-element.18.column_ref, f32[5,125,1024]{2,1,0:T(8,128)S(1)} %rim.1.base_ref), custom_call_target="tpu_custom_call" | custom-call | tf_op jit(solution)/shard_map/last/pallas_call | solution.py:642
Async XLA Ops:
  1.8 7.6 %all-to-all-start = ((f32[8,8,128]{2,1,0:T(8,128)}), f32[8,8,128]{2,1,0:T(8,128)S(1)}, u32[]{:S(2)}, u32[]{:S(2)}) async-start(f32[8,8,128]{2,1,0:T(8,128)} %ids.1), calls=%async_computation | async-start | bytes 65536 | tf_op jit(solution)/shard_map/all_to_all | solution.py:479
  13.0 11.5 %all-to-all-start.1 = ((f32[8,11,8,128]{3,2,1,0:T(8,128)}), f32[8,11,8,128]{3,2,1,0:T(8,128)S(1)}, u32[]{:S(2)}, u32[]{:S(2)}) async-start(f32[8,11,8,128]{3,2,1,0:T(8,128)} %get-tuple-element.15), calls=%async_computation.1 | async-start | bytes 720896 | tf_op jit(solution)/shard_map/all_to_all | solution.py:479
  24.5 10.5 %copy-start = (f32[5,32,128]{2,1,0:T(8,128)S(1)}, f32[5,32,128]{2,1,0:T(8,128)}, u32[]{:S(2)}) copy-start(f32[5,32,128]{2,1,0:T(8,128)} %get-tuple-element.17._) | copy-start | bytes 245764
  28.8 13.4 %all-to-all-start.2 = ((f32[8,5,8,128]{3,2,1,0:T(8,128)}), f32[8,5,8,128]{3,2,1,0:T(8,128)S(1)}, u32[]{:S(2)}, u32[]{:S(2)}) async-start(f32[8,5,8,128]{3,2,1,0:T(8,128)} %cut.1), calls=%async_computation.2 | async-start | bytes 327680 | tf_op jit(solution)/shard_map/all_to_all | solution.py:479
  33.4 6.0 %collective-permute-start = (f32[5,32,128]{2,1,0:T(8,128)S(1)}, f32[5,32,128]{2,1,0:T(8,128)S(1)}, u32[]{:S(2)}, u32[]{:S(2)}) collective-permute-start(f32[5,32,128]{2,1,0:T(8,128)S(1)} %get-tuple-element.19), channel_id=1, source_target_pairs={{0,8},{16,24},{8,0},{24,16},{1,9},{17,25},{9,1},{25,17},{2,10},{18... | collective-permute-start | bytes 245768 | tf_op jit(solution)/shard_map/ppermute | solution.py:475
  35.0 6.3 %collective-permute-start.1 = (f32[5,32,128]{2,1,0:T(8,128)S(1)}, f32[5,32,128]{2,1,0:T(8,128)S(1)}, u32[]{:S(2)}, u32[]{:S(2)}) collective-permute-start(f32[5,32,128]{2,1,0:T(8,128)S(1)} %copy-done), channel_id=1, source_target_pairs={{8,16},{16,8},{9,17},{17,9},{10,18},{18,10},{11,19},{19,11},{12,20... | collective-permute-start | bytes 245768 | tf_op jit(solution)/shard_map/ppermute | solution.py:475

commit v3 on v2

--- a/solution.py
+++ b/solution.py
@@ -6,6 +6,7 @@
 from jax.experimental import pallas as pl
 from jax.experimental.pallas import tpu as pltpu
 from jax.sharding import PartitionSpec as P
+
 
 DEGREE = 4
 LAYERS = 8
@@ -117,7 +118,9 @@
 
 
 def load_kernel(
-    covered_hbm, state_hbm, state_ref, first_ref, second_ref, rows_ref, column_ref, covered_ref, acc_ref, sems
+    covered_hbm, state_hbm, operator_hbm, flux_hbm, penalty_hbm,
+    state_ref, first_ref, second_ref, rows_ref, column_ref, operator_ref, flux_ref, penalty_ref,
+    covered_ref, acc_ref, sems,
 ):
     even = lax.axis_index("px") % 2 == 0
     nvar, modes, elems = state_ref.shape
@@ -127,6 +130,14 @@
     covered_copy = pltpu.make_async_copy(covered_hbm, covered_ref, sems.at[nvar])
     covered_copy.start()
     for copy in copies:
+        copy.start()
+    small = [
+        pltpu.make_async_copy(source, target, sems.at[nvar + 1 + index])
+        for index, (source, target) in enumerate(
+            ((operator_hbm, operator_ref), (flux_hbm, flux_ref), (penalty_hbm, penalty_ref))
+        )
+    ]
+    for copy in small:
         copy.start()
     acc_ref[...] = jnp.zeros_like(acc_ref)
     first_ref[...] = jnp.zeros_like(first_ref)
@@ -152,9 +163,11 @@
             found = jnp.where((spots + LANES) // LANES == layer + 1, picked, found)
         acc_ref[var, :modes] = found
         rows_ref[var] = acc_ref[var].T
-
-
-def pick_kernel(cap, share, got_ref, state_ref, old_hbm, out_ref, column_ref, old_ref, acc_ref, sems):
+    for copy in small:
+        copy.wait()
+
+
+def pick_kernel(cap, got_ref, state_ref, old_hbm, out_hbm, column_ref, out_ref, old_ref, acc_ref, sems):
     nvar, modes, elems = state_ref.shape
     peers = got_ref.shape[0]
     half = LANES // 2
@@ -183,8 +196,15 @@
     data = got_ref[0]
     for peer in range(1, peers):
         data = data + got_ref[peer]
+    sent = []
+
+    def send(kind):
+        sent.append(pltpu.make_async_copy(out_ref.at[:, kind], out_hbm.at[:, kind], sems.at[nvar + kind]))
+        sent[-1].start()
+
     for peer in range(peers):
         out_ref[peer, 2 * nvar, :, :] = data
+    send(2 * nvar)
     column = jnp.broadcast_to(row, (LANES, LANES)).T.astype(jnp.int32)
     if cap < SUBS:
         column_ref[...] = jnp.zeros_like(column_ref) - 1
@@ -200,12 +220,18 @@
                 if cap < SUBS:
                     out_ref[peer, kind * nvar + var] = jnp.zeros((SUBS, LANES), F32)
                 out_ref[peer, kind * nvar + var, :cap] = rows[first : first + cap]
+        send(var)
+        send(nvar + var)
+    for copy in sent:
+        copy.wait()
 
 
 def main_kernel(
-    flux_hbm, penalty_hbm, jac_hbm, operator_hbm, state_hbm, old_hbm, _,
-    out_ref, _unused, flux_ref, penalty_ref, jac_ref, state_ref, old_ref, operator_ref, padded_ref, matrix_ref, right_ref, product_ref, face_ref, sems,
+    flux_vmem, penalty_vmem, operator_ref, _, jac_hbm, old_hbm, owner_hbm, _rim,
+    out_ref, owner_ref, _same, flux_ref, penalty_ref, jac_ref, old_ref, padded_ref, matrix_ref, right_ref,
+    product_ref, face_ref, sems,
 ):
+    state_ref = out_ref
     nvar, modes, elems = state_ref.shape
     degree_one = DEGREE + 1
     face = modes // degree_one
@@ -215,17 +241,17 @@
         pltpu.make_async_copy(source, target, sems.at[index])
         for index, (source, target) in enumerate(
             (
-                (operator_hbm, operator_ref),
-                (state_hbm, state_ref),
+                (flux_vmem, flux_ref),
+                (penalty_vmem, penalty_ref),
                 (old_hbm, old_ref),
-                (flux_hbm, flux_ref),
-                (penalty_hbm, penalty_ref),
                 (jac_hbm, jac_ref),
+                (owner_hbm, owner_ref),
             )
         )
     ]
-    for index in (3, 4, 0, 1, 5):
-        copies[index].start()
+    for copy in copies:
+        copy.start()
+    chunks = elems // width
     padded_ref[...] = jnp.zeros_like(padded_ref)
     gap = LANES - modes
     for var in range(nvar):
@@ -244,9 +270,8 @@
     inside = iota((LANES, LANES), 0) < modes
     own_face = jnp.where((row_low == col_low) & (apart == 0.0) & inside, 2.0, 0.0)
     own_face = jnp.where(iota((LANES, LANES), 1) < modes, own_face, 0.0)
-    for index in (3, 4, 0):
-        copies[index].wait()
-    copies[2].start()
+    copies[0].wait()
+    copies[1].wait()
     padded_ref[:, :modes, :modes] = operator_ref[...]
     for var in range(nvar):
         for other in range(nvar):
@@ -276,14 +301,12 @@
             matrix_ref[:, 2 * size :], right_ref[chunk % 2, :size]
         )
 
-    copies[1].wait()
     split(0)
     multiply(0)
     split(1)
-    copies[5].wait()
     copies[2].wait()
+    copies[3].wait()
     below = [jnp.zeros((face, LANES), F32)] * nvar
-    chunks = elems // width
     for chunk in range(chunks):
         first = chunk * width
         lanes = slice(first, first + width)
@@ -309,16 +332,17 @@
             out_ref[var, :, lanes] = (
                 product_ref[chunk % 2, var * LANES : var * LANES + modes] + scale * change
             ) - face_ref[var, :modes]
+    copies[4].wait()
 
 
 def cut_kernel(
-    owner_hbm, got_ref, mass_hbm, operator_hbm, _, out_ref, owner_ref, mass_ref, operator_ref, left_ref, term_ref,
+    owner_vmem, got_ref, mass_hbm, operator_hbm, out_ref, owner_ref, mass_ref, operator_ref, left_ref, term_ref,
     spot_ref, seen_ref, sems,
 ):
     groups, modes = mass_ref.shape[:2]
     peers, nvar = out_ref.shape[0], out_ref.shape[1]
     kinds = got_ref.shape[1]
-    owner_copy = pltpu.make_async_copy(owner_hbm, owner_ref, sems.at[0, groups])
+    owner_copy = pltpu.make_async_copy(owner_vmem, owner_ref, sems.at[0, groups])
     owner_copy.start()
     copies = []
     for group in range(groups):
@@ -357,8 +381,8 @@
         for inner in range(SUBS):
             index = group * SUBS + inner
             blocks = []
-            for ref in (mass_ref, operator_ref):
-                block = ref.at[group].reshape(modes * SUBS, modes)[pl.ds(inner, modes, stride=SUBS), :]
+            for ref in (mass_ref.at[group], operator_ref.at[group]):
+                block = ref.reshape(modes * SUBS, modes)[pl.ds(inner, modes, stride=SUBS), :]
                 blocks.append(jnp.concatenate([block, zero], axis=1))
             high, low = halves(jnp.concatenate(blocks, axis=1))
             left = left_ref[index].astype(BF16)
@@ -368,10 +392,21 @@
         out[pl.ds(spot_ref[index], nvar, stride=SUBS), :modes] = term_ref[index, :nvar, :modes]
 
 
-def body_kernel(bodies, count, share, got_ref, rows_ref, column_ref, base_ref, out_ref, data_ref, basis_ref, lift_ref, left_ref):
+def body_kernel(
+    bodies, count, share, got_ref, rows_hbm, column_hbm, base_ref, out_ref,
+    rows_ref, column_ref, data_ref, basis_ref, lift_ref, left_ref, sems,
+):
     peers = got_ref.shape[0]
     nvar, modes, elems = out_ref.shape
     degree_one = DEGREE + 1
+    copies = [
+        pltpu.make_async_copy(source, target, sems.at[index])
+        for index, (source, target) in enumerate(
+            ((rows_hbm, rows_ref), (column_hbm, column_ref))
+        )
+    ]
+    for copy in copies:
+        copy.start()
     for peer in range(peers):
         data_ref[peer * share : (peer + 1) * share] = got_ref[peer, 2 * nvar, 1 : 1 + share]
     lift_ref[...] = jnp.zeros_like(lift_ref)
@@ -398,6 +433,7 @@
         basis_ref[0, body], basis_ref[1, body] = halves(basis)
     bases = [(basis_ref[0, body], basis_ref[1, body]) for body in range(bodies)]
     traces = []
+    copies[0].wait()
     for body in range(bodies):
         rows = jnp.concatenate([rows_ref[var, body * count : (body + 1) * count] for var in range(nvar)], axis=0)
         traces.append(product(halves(rows), bases[body]))
@@ -419,6 +455,7 @@
         left_ref[var * LANES : (var + 1) * LANES, LANES:] = low
 
     width = 2 * LANES
+    copies[1].wait()
     spots = jnp.concatenate([column_ref[...]] * (width // LANES), axis=1)
     for first in range(0, elems, width):
         chosen = (spots == iota((LANES, width), 1) + first).astype(BF16)
@@ -446,25 +483,20 @@
         out_ref[var, :, top] = base_ref[var, :, top] - face_ref[1, var, :modes]
 
 
-def last_kernel(got_ref, column_ref, base_ref, out_hbm, out_ref, left_ref, sems):
+def last_kernel(got_ref, column_ref, base_ref, out_hbm, out_ref, chosen_ref, sems):
     nvar, modes, elems = out_ref.shape
     slots = column_ref.shape[0]
-    width = 2 * LANES
-    for var in range(nvar):
-        rows = got_ref[:, var].reshape(slots, LANES).T
-        left_ref[var * LANES : (var + 1) * LANES] = jnp.concatenate(halves(rows), axis=1)
-    spots = jnp.concatenate([column_ref[...]] * (width // LANES), axis=1)
+    for layer in range(elems // LANES):
+        lanes = slice(layer * LANES, (layer + 1) * LANES)
+        chosen = (column_ref[...] == iota((slots, LANES), 1) + layer * LANES).astype(BF16)
+        chosen_ref[:slots, lanes] = chosen
+        chosen_ref[slots:, lanes] = chosen
     copies = []
-    for start in range(0, elems, width):
-        lanes = slice(start, start + width)
-        chosen = (spots == iota((slots, width), 1) + start).astype(BF16)
-        added = mxu(left_ref[...], jnp.concatenate([chosen, chosen], axis=0))
-        for var in range(nvar):
-            out_ref[var, :, lanes] = base_ref[var, :, lanes] + added[var * LANES : var * LANES + modes]
-            copies.append(
-                pltpu.make_async_copy(out_ref.at[var, :, lanes], out_hbm.at[var, :, lanes], sems.at[len(copies)])
-            )
-            copies[-1].start()
+    for var in range(nvar):
+        left = jnp.concatenate(halves(got_ref[:, var].reshape(slots, LANES).T), axis=1)
+        out_ref[var] = base_ref[var] + mxu(left, chosen_ref[...])[:modes]
+        copies.append(pltpu.make_async_copy(out_ref.at[var], out_hbm.at[var], sems.at[var]))
+        copies[-1].start()
     for copy in copies:
         copy.wait()
 
@@ -519,78 +551,91 @@
     stack = shaped((nvar, LANES, LANES), F32)
     square = shaped((LANES, LANES), jnp.int32)
     scratch = pltpu.VMEM(stack.shape, F32)
-    state, first_rim, second_rim, covered_rows, covered_column = pl.pallas_call(
+    flux = in_hbm(flux_jacobian_list.transpose(1, 0, 2))
+    state, first_rim, second_rim, covered_rows, covered_column, operator, flux, penalties = pl.pallas_call(
         load_kernel,
         grid=(1,),
-        out_shape=(field, face_rows, stored(face_rows), stored(stack), stored(square)),
-        in_specs=[remote(), remote()],
-        out_specs=(kept(), whole(face_rows), whole(face_rows), whole(stack), whole(square)),
+        out_shape=(
+            field,
+            face_rows,
+            stored(face_rows),
+            stored(stack),
+            stored(square),
+            pltpu.VMEM(volume_operator_list.shape, F32),
+            pltpu.VMEM(flux.shape, F32),
+            pltpu.VMEM(penalty.shape, F32),
+        ),
+        in_specs=[remote()] * 5,
+        out_specs=(kept(), whole(face_rows), whole(face_rows), whole(stack), whole(square)) + (kept(),) * 3,
         scratch_shapes=[
             pltpu.VMEM(covered.shape, jnp.int32),
             scratch,
-            pltpu.SemaphoreType.DMA((nvar + 1,)),
+            pltpu.SemaphoreType.DMA((nvar + 4,)),
         ],
         compiler_params=params(4),
         name="load",
-    )(in_hbm(covered), in_hbm(current_state))
+    )(in_hbm(covered), in_hbm(current_state), in_hbm(volume_operator_list), flux, in_hbm(penalty))
     first_rim = swap(first_rim, "px", 0)
 
     reply = shaped((peers, 2 * nvar + 1, SUBS, LANES), F32)
     column = shaped((slots, LANES), jnp.int32)
     states_out, slot_column = pl.pallas_call(
-        functools.partial(pick_kernel, cap, share),
+        functools.partial(pick_kernel, cap),
         grid=(1,),
-        out_shape=(pltpu.VMEM(reply.shape, F32), pltpu.VMEM(column.shape, column.dtype)),
+        out_shape=(stored(reply), pltpu.VMEM(column.shape, column.dtype)),
         in_specs=[kept(), kept(), remote()],
-        out_specs=(kept(), kept()),
-        scratch_shapes=[pltpu.VMEM(current_state.shape, F32), scratch, pltpu.SemaphoreType.DMA((nvar,))],
+        out_specs=(remote(), kept()),
+        scratch_shapes=[
+            pltpu.VMEM(reply.shape, F32),
+            pltpu.VMEM(current_state.shape, F32),
+            scratch,
+            pltpu.SemaphoreType.DMA((3 * nvar + 1,)),
+        ],
         compiler_params=params(6),
         name="pick",
     )(requests, in_vmem(state), in_hbm(state_old))
     replies = exchange(states_out)
 
     jacobian_row = in_hbm(jacobian.reshape(1, elems))
-    residual, second_rim = pl.pallas_call(
+    groups = cuts // SUBS
+    mass_cols, operator_cols = in_hbm(cut_mass.transpose(1, 0, 2)), in_hbm(cut_operator.transpose(1, 0, 2))
+    residual, owner_row, second_rim = pl.pallas_call(
         main_kernel,
         grid=(1,),
-        out_shape=(field, stored(face_rows)),
-        in_specs=[remote()] * 7,
-        out_specs=(kept(), remote()),
+        out_shape=(field, pltpu.VMEM((cuts,), jnp.int32), stored(face_rows)),
+        in_specs=[kept()] * 4 + [remote()] * 4,
+        out_specs=(kept(), kept(), remote()),
         scratch_shapes=[
             pltpu.SMEM((nvar, 3, nvar), F32),
             pltpu.SMEM((nvar,), F32),
             pltpu.VMEM((1, elems), F32),
             pltpu.VMEM(current_state.shape, F32),
-            pltpu.VMEM(current_state.shape, F32),
-            pltpu.VMEM(volume_operator_list.shape, F32),
             pltpu.VMEM((3, LANES, LANES), F32),
             pltpu.VMEM((size, 3 * size), BF16),
             pltpu.VMEM((2, 2 * size, wide), BF16),
             pltpu.VMEM((2, size, wide), F32),
             pltpu.VMEM((nvar, LANES, wide), F32),
-            pltpu.SemaphoreType.DMA((6,)),
+            pltpu.SemaphoreType.DMA((5,)),
         ],
-        input_output_aliases={6: 1},
+        input_output_aliases={3: 0, 7: 2},
         compiler_params=params(20),
         cost_estimate=pl.CostEstimate(
             flops=6 * size * size * elems, transcendentals=0, bytes_accessed=4 * 4 * nvar * modes * elems
         ),
         name="main",
     )(
-        in_hbm(flux_jacobian_list.transpose(1, 0, 2)), in_hbm(penalty), jacobian_row,
-        in_hbm(volume_operator_list), in_hbm(current_state), in_hbm(state_old), in_hbm(second_rim),
+        in_vmem(flux), in_vmem(penalties), in_vmem(operator), in_vmem(state), jacobian_row, in_hbm(state_old),
+        in_hbm(cut_owner.reshape(cuts)), in_hbm(second_rim),
     )
-    after_main = second_rim
     second_rim = swap(second_rim, "px", 1)
 
     terms = shaped((peers, nvar, SUBS, LANES), F32)
-    groups = cuts // SUBS
     blocks = pltpu.VMEM((groups, modes, SUBS, modes), F32)
     results_out = pl.pallas_call(
         cut_kernel,
         grid=(1,),
         out_shape=pltpu.VMEM(terms.shape, F32),
-        in_specs=[remote(), kept(), remote(), remote(), remote()],
+        in_specs=[kept(), kept(), remote(), remote()],
         out_specs=kept(),
         scratch_shapes=[
             pltpu.SMEM((cuts,), jnp.int32),
@@ -605,8 +650,7 @@
         compiler_params=params(10),
         name="cut",
     )(
-        in_hbm(cut_owner.reshape(cuts)), replies,
-        in_hbm(cut_mass.transpose(1, 0, 2)), in_hbm(cut_operator.transpose(1, 0, 2)), in_hbm(after_main),
+        in_vmem(owner_row), replies, mass_cols, operator_cols,
     )
     results = exchange(results_out)
 
@@ -614,13 +658,16 @@
         functools.partial(body_kernel, bodies, count, share),
         grid=(1,),
         out_shape=field,
-        in_specs=[kept(), whole(stack), whole(square), kept()],
+        in_specs=[kept(), remote(), remote(), kept()],
         out_specs=kept(),
         scratch_shapes=[
+            scratch,
+            pltpu.VMEM(square.shape, jnp.int32),
             pltpu.VMEM((pad8(peers * share), LANES), F32),
             pltpu.VMEM((2, bodies, LANES, LANES), BF16),
             scratch,
             pltpu.VMEM((size, wide), BF16),
+            pltpu.SemaphoreType.DMA((2,)),
         ],
         input_output_aliases={3: 0},
         compiler_params=params(6),
@@ -647,8 +694,8 @@
         out_specs=remote(),
         scratch_shapes=[
             pltpu.VMEM(current_state.shape, F32),
-            pltpu.VMEM((size, 2 * slots), BF16),
-            pltpu.SemaphoreType.DMA((nvar * (elems // wide),)),
+            pltpu.VMEM((2 * slots, elems), BF16),
+            pltpu.SemaphoreType.DMA((nvar,)),
         ],
         compiler_params=params(8),
         name="last",
@@ -674,6 +721,5 @@
         P(both, None),
         P(both, None),
     )
-    return jax.shard_map(
-        local, mesh=mesh, in_specs=in_specs, out_specs=P(None, None, both), check_vma=False
-    )
+
+    return jax.shard_map(local, mesh=mesh, in_specs=in_specs, out_specs=P(None, None, both), check_vma=False)

time: 44.9 us -> 44.4 us (0.989)
  Pallas kernels: 25.1 us -> 23.8 us
  waiting for transfers between devices: 1.99 us -> 2.62 us
    pallas_call x2, Pallas kernels: 10.2 us -> 9.05 us  [the longest x1 5.69 us: local(): pl.pallas_call(main_kernel, grid=(1,), out_shape=(field, pltpu.VMEM((cuts...]
    all_to_all x3, waiting for transfers between devices: 0.11 us -> 0.85 us  [exchange(): return lax.all_to_all(value, 'py', split_axis=0, concat_axis=0, tiled=True)]
  transfers between devices with their start and end apart: 5 -> 5, of which waited for: 2 -> 2; matrix products, arithmetic and copies ran while one was open for 0% -> 0% of each run, Pallas kernels for 30% -> 29%
where the time goes in v3:
time: 44.4 us; the launch traced here: 43.9 us
  Pallas kernels  23.8 us (54%)
  starting transfers between devices  17.3 us (39%)
  waiting for transfers between devices  2.62 us (6%)
    all_to_all x3, starting transfers between devices, exchange(): return lax.all_to_all(value, 'py', split_axis=0, concat_axis=0, tiled=True)  13.9 us
    pallas_call x1, Pallas kernels, local(): pl.pallas_call(main_kernel, grid=(1,), out_shape=(field, pltpu.VMEM((cuts...  5.69 us
    pallas_call x1, Pallas kernels, local(): pl.pallas_call(cut_kernel, grid=(1,), out_shape=pltpu.VMEM(terms.shape, F...  4.27 us
    ppermute x2, starting transfers between devices, swap(): lax.ppermute(value, axis, pairs + [(high, low) for low, high in pairs])  3.49 us
    pallas_call x1, Pallas kernels, local(): pl.pallas_call(functools.partial(pick_kernel, cap), grid=(1,), out_shape=...  3.36 us
    pallas_call x1, Pallas kernels, local(): pl.pallas_call(load_kernel, grid=(1,), out_shape=(field, face_rows, store...  3.34 us
    pallas_call x1, Pallas kernels, local(): pl.pallas_call(functools.partial(body_kernel, bodies, count, share), grid...  2.63 us
    pallas_call x1, Pallas kernels, local(): pl.pallas_call(last_kernel, grid=(1,), out_shape=shaped(current_state.sha...  1.89 us
  transfers between devices with their start and end apart: 5, of which 2 were waited for; matrix products, arithmetic and copies ran while one was open for 0% of the time, Pallas kernels for 29%

profile of v3, /device:TPU:18, one launch (start us, length us, event | category | flops | bytes accessed | tf_op | source)
XLA Modules:
  0.0 43.9 jit_solution(1055016808779453123)
XLA Ops:
  0.0 1.8 %ids.1 = f32[8,8,128]{2,1,0:T(8,128)} custom-call(s32[6]{0:T(128)} %hold_ref.1, s32[1,40]{1,0:T(1,128)} %bitcast.11, s32[1,40]{1,0:T(1,128)} %bitcast.10, f32[6,3,128]{2,1,0:T(4,128)} %points_ref.1, f32[6,3,128]{2,1,0:T(4,128)} %normals_ref.1, f32[6,128]{1,0:T(8,128)} %weights_ref.1), custom_call_target="tpu_custom_call" | custom-call | tf_op jit(solution)/shard_map/ids/pallas_call | solution.py:537
  1.8 4.3 %all-to-all-start = ((f32[8,8,128]{2,1,0:T(8,128)}), f32[8,8,128]{2,1,0:T(8,128)S(1)}, u32[]{:S(2)}, u32[]{:S(2)}) async-start(f32[8,8,128]{2,1,0:T(8,128)} %ids.1), calls=%async_computation | async-start | bytes 65536 | tf_op jit(solution)/shard_map/all_to_all | solution.py:511
  6.0 3.3 %load.1 = (f32[5,125,1024]{2,1,0:T(8,128)S(1)}, f32[5,32,128]{2,1,0:T(8,128)S(1)}, f32[5,32,128]{2,1,0:T(8,128)}, f32[5,128,128]{2,1,0:T(8,128)}, s32[128,128]{1...) custom-call(s32[6,16]{1,0:T(8,128)} %covered_hbm.1, f32[5,125,1024]{2,1,0:T(8,128)} %state_hbm.1, ...), custom_call_target="tpu_custom_call" | custom-call | tf_op jit(solution)/shard_map/load/pallas_call | solution.py:555
  9.4 0.0 all-to-all-done.got_ref
  9.4 3.4 %pick.1 = (f32[8,11,8,128]{3,2,1,0:T(8,128)}, s32[64,128]{1,0:T(8,128)S(1)}) custom-call(f32[8,8,128]{2,1,0:T(8,128)S(1)} %all-to-all-done.got_ref, f32[5,125,1024]{2,1,0:T(8,128)S(1)} %get-tuple-element.21._.state_ref, f32[5,125,1024]{2,1,0:T(8,128)} %old_hbm.3), custom_call_target="tpu_custom_call" | custom-call | tf_op jit(solution)/shard_map/pick/pallas_call | solution.py:582
  12.8 4.8 %all-to-all-start.1 = ((f32[8,11,8,128]{3,2,1,0:T(8,128)}), f32[8,11,8,128]{3,2,1,0:T(8,128)S(1)}, u32[]{:S(2)}, u32[]{:S(2)}) async-start(f32[8,11,8,128]{3,2,1,0:T(8,128)} %get-tuple-element.24), calls=%async_computation.1 | async-start | bytes 720896 | tf_op jit(solution)/shard_map/all_to_all | solution.py:511
  17.6 5.7 %main.1 = (f32[5,125,1024]{2,1,0:T(8,128)S(1)}, s32[40]{0:T(128)S(1)}, f32[5,32,128]{2,1,0:T(8,128)}) custom-call(f32[5,3,5]{2,1,0:T(4,128)S(1)} %get-tuple-element.18.flux_vmem, f32[5]{0:T(128)S(1)} %get-tuple-element.19.penalty_vmem, f32[3,125,125]{2,1,0:T(8,128)S(1)} %get-tuple-element.20.operator_ref, ...), custom_call_target="tpu_custom_call", output_to_operand_aliasing={{0}: (3, {}), {2}: (7, {})} | custom-call | flops 2516582400 | bytes 10240000 | tf_op jit(solution)/shard_map/main/pallas_call | solution.py:602
  23.3 0.8 %all-to-all-done.1.got_ref = f32[8,11,8,128]{3,2,1,0:T(8,128)S(1)} async-done(((f32[8,11,8,128]{3,2,1,0:T(8,128)}), f32[8,11,8,128]{3,2,1,0:T(8,128)S(1)}, u32[]{:S(2)}, u32[]{:S(2)}) %all-to-all-start.1) | async-done | bytes 360480 | tf_op jit(solution)/shard_map/all_to_all | solution.py:511
  24.1 0.0 copy-start
  24.1 4.3 %cut.1 = f32[8,5,8,128]{3,2,1,0:T(8,128)} custom-call(s32[40]{0:T(128)S(1)} %get-tuple-element.23.owner_vmem, f32[8,11,8,128]{3,2,1,0:T(8,128)S(1)} %all-to-all-done.1.got_ref, f32[125,40,125]{2,1,0:T(8,128)} %bitcast.7, f32[125,40,125]{2,1,0:T(8,128)} %bitcast.8), custom_call_target="tpu_custom_call" | custom-call | tf_op jit(solution)/shard_map/cut/pallas_call | solution.py:634
  28.4 4.8 %all-to-all-start.2 = ((f32[8,5,8,128]{3,2,1,0:T(8,128)}), f32[8,5,8,128]{3,2,1,0:T(8,128)S(1)}, u32[]{:S(2)}, u32[]{:S(2)}) async-start(f32[8,5,8,128]{3,2,1,0:T(8,128)} %cut.1), calls=%async_computation.2 | async-start | bytes 327680 | tf_op jit(solution)/shard_map/all_to_all | solution.py:511
  33.2 1.6 %collective-permute-start = (f32[5,32,128]{2,1,0:T(8,128)S(1)}, f32[5,32,128]{2,1,0:T(8,128)S(1)}, u32[]{:S(2)}, u32[]{:S(2)}) collective-permute-start(f32[5,32,128]{2,1,0:T(8,128)S(1)} %get-tuple-element.26), channel_id=1, source_target_pairs={{0,8},{16,24},{8,0},{24,16},{1,9},{17,25},{9,1},{25,17},{2,10},{18... | collective-permute-start | bytes 245768 | tf_op jit(solution)/shard_map/ppermute | solution.py:507
  34.8 0.0 copy-done
  34.8 1.9 %collective-permute-start.1 = (f32[5,32,128]{2,1,0:T(8,128)S(1)}, f32[5,32,128]{2,1,0:T(8,128)S(1)}, u32[]{:S(2)}, u32[]{:S(2)}) collective-permute-start(f32[5,32,128]{2,1,0:T(8,128)S(1)} %copy-done), channel_id=1, source_target_pairs={{8,16},{16,8},{9,17},{17,9},{10,18},{18,10},{11,19},{19,11},{12,20... | collective-permute-start | bytes 245768 | tf_op jit(solution)/shard_map/ppermute | solution.py:507
  36.7 2.6 %body.1.base_ref = f32[5,125,1024]{2,1,0:T(8,128)S(1)} custom-call(f32[8,11,8,128]{3,2,1,0:T(8,128)S(1)} %all-to-all-done.1.got_ref, f32[5,128,128]{2,1,0:T(8,128)} %get-tuple-element.28.rows_hbm, s32[128,128]{1,0:T(8,128)} %get-tuple-element.29.column_hbm, f32[5,125,1024]{2,1,0:T(8,128)S(1)} %get-tuple-element.30.base_ref), custom_call_target="tpu_custom_call", output_to_operand_aliasing={{}: (3, {})} | custom-call | tf_op jit(solution)/shard_map/body/pallas_call | solution.py:657
  39.3 0.0 collective-permute-done.first_ref
  39.3 1.8 %collective-permute-done.1.second_ref = f32[5,32,128]{2,1,0:T(8,128)S(1)} collective-permute-done((f32[5,32,128]{2,1,0:T(8,128)S(1)}, f32[5,32,128]{2,1,0:T(8,128)S(1)}, u32[]{:S(2)}, u32[]{:S(2)}) %collective-permute-start.1) | collective-permute-done | bytes 81952 | tf_op jit(solution)/shard_map/ppermute | solution.py:507
  41.1 0.9 %rim.1.base_ref = f32[5,125,1024]{2,1,0:T(8,128)S(1)} custom-call(f32[5]{0:T(128)} %penalty_ref.1, f32[5,32,128]{2,1,0:T(8,128)S(1)} %collective-permute-done.first_ref, f32[5,32,128]{2,1,0:T(8,128)S(1)} %collective-permute-done.1.second_ref, f32[5,125,1024]{2,1,0:T(8,128)S(1)} %body.1.base_ref), custom_call_target="tpu_custom_call", output_to_operand_aliasing={{}: (3, {})} | custom-call | tf_op jit(solution)/shard_map/rim/pallas_call | solution.py:677
  42.0 0.0 all-to-all-done.2.got_ref
  42.0 1.9 %last.1 = f32[5,125,1024]{2,1,0:T(8,128)} custom-call(f32[8,5,8,128]{3,2,1,0:T(8,128)S(1)} %all-to-all-done.2.got_ref, s32[64,128]{1,0:T(8,128)S(1)} %get-tuple-element.25.column_ref, f32[5,125,1024]{2,1,0:T(8,128)S(1)} %rim.1.base_ref), custom_call_target="tpu_custom_call" | custom-call | tf_op jit(solution)/shard_map/last/pallas_call | solution.py:689
Async XLA Ops:
  1.8 7.6 %all-to-all-start = ((f32[8,8,128]{2,1,0:T(8,128)}), f32[8,8,128]{2,1,0:T(8,128)S(1)}, u32[]{:S(2)}, u32[]{:S(2)}) async-start(f32[8,8,128]{2,1,0:T(8,128)} %ids.1), calls=%async_computation | async-start | bytes 65536 | tf_op jit(solution)/shard_map/all_to_all | solution.py:511
  12.8 11.3 %all-to-all-start.1 = ((f32[8,11,8,128]{3,2,1,0:T(8,128)}), f32[8,11,8,128]{3,2,1,0:T(8,128)S(1)}, u32[]{:S(2)}, u32[]{:S(2)}) async-start(f32[8,11,8,128]{3,2,1,0:T(8,128)} %get-tuple-element.24), calls=%async_computation.1 | async-start | bytes 720896 | tf_op jit(solution)/shard_map/all_to_all | solution.py:511
  24.1 10.6 %copy-start = (f32[5,32,128]{2,1,0:T(8,128)S(1)}, f32[5,32,128]{2,1,0:T(8,128)}, u32[]{:S(2)}) copy-start(f32[5,32,128]{2,1,0:T(8,128)} %get-tuple-element.27) | copy-start | bytes 245764
  28.4 13.6 %all-to-all-start.2 = ((f32[8,5,8,128]{3,2,1,0:T(8,128)}), f32[8,5,8,128]{3,2,1,0:T(8,128)S(1)}, u32[]{:S(2)}, u32[]{:S(2)}) async-start(f32[8,5,8,128]{3,2,1,0:T(8,128)} %cut.1), calls=%async_computation.2 | async-start | bytes 327680 | tf_op jit(solution)/shard_map/all_to_all | solution.py:511
  33.2 6.1 %collective-permute-start = (f32[5,32,128]{2,1,0:T(8,128)S(1)}, f32[5,32,128]{2,1,0:T(8,128)S(1)}, u32[]{:S(2)}, u32[]{:S(2)}) collective-permute-start(f32[5,32,128]{2,1,0:T(8,128)S(1)} %get-tuple-element.26), channel_id=1, source_target_pairs={{0,8},{16,24},{8,0},{24,16},{1,9},{17,25},{9,1},{25,17},{2,10},{18... | collective-permute-start | bytes 245768 | tf_op jit(solution)/shard_map/ppermute | solution.py:507
  34.8 6.3 %collective-permute-start.1 = (f32[5,32,128]{2,1,0:T(8,128)S(1)}, f32[5,32,128]{2,1,0:T(8,128)S(1)}, u32[]{:S(2)}, u32[]{:S(2)}) collective-permute-start(f32[5,32,128]{2,1,0:T(8,128)S(1)} %copy-done), channel_id=1, source_target_pairs={{8,16},{16,8},{9,17},{17,9},{10,18},{18,10},{11,19},{19,11},{12,20... | collective-permute-start | bytes 245768 | tf_op jit(solution)/shard_map/ppermute | solution.py:507
